TPU v7x, 32 devices: a whole 2x2x4 slice. The times are simulated.
32 devices in a mesh: grp: 4 (over y, core), fsdp: 8 (over z, x).
Axes of the slice: x: 2, y: 2, z: 4, core: 2. Of those that a mesh axis runs over, the one named last changes fastest.
Arguments:
- tokens: bfloat16 [64, 512, 768], P('grp', 'fsdp'), may hold values from -6 to 6
- frames: bfloat16 [64, 1536, 768], P('grp', 'fsdp'), may hold values from -6 to 6
- lengths: int32 [64], P('grp'), may hold values from 1 to 448, as said below
- cotangent: bfloat16 [64, 512, 768], P('grp', 'fsdp'), may hold values from -6 to 6
- self_in: bfloat16 [768, 2304], P(('grp', 'fsdp')), may hold values from -0.21875 to 0.21875
- self_out: bfloat16 [768, 768], P(('grp', 'fsdp')), may hold values from -1.75 to 1.75
- cross_q: bfloat16 [768, 768], P(('grp', 'fsdp')), may hold values from -0.21875 to 0.21875
- cross_kv: bfloat16 [768, 1536], P(('grp', 'fsdp')), may hold values from -0.21875 to 0.21875
- cross_out: bfloat16 [768, 768], P(('grp', 'fsdp')), may hold values from -1.75 to 1.75
- fc_in: bfloat16 [768, 3072], P(('grp', 'fsdp')), may hold values from -0.21875 to 0.21875
- fc_out: bfloat16 [3072, 768], P(('grp', 'fsdp')), may hold values from -0.109375 to 0.109375
- norm_gain: bfloat16 [768, 4], P(('grp', 'fsdp')), may hold values from 0.25 to 1.75
- norm_bias: bfloat16 [768, 4], P(('grp', 'fsdp')), may hold values from -3 to 3
Outputs:
- output: bfloat16 [64, 512, 768], P('grp', 'fsdp')
- grad_tokens: bfloat16 [64, 512, 768], P('grp', 'fsdp')
- grad_frames: bfloat16 [64, 1536, 768], P('grp', 'fsdp')
- grad_self_in: float32 [768, 2304], P(('grp', 'fsdp'))
- grad_self_out: float32 [768, 768], P(('grp', 'fsdp'))
- grad_cross_q: float32 [768, 768], P(('grp', 'fsdp'))
- grad_cross_kv: float32 [768, 1536], P(('grp', 'fsdp'))
- grad_cross_out: float32 [768, 768], P(('grp', 'fsdp'))
- grad_fc_in: float32 [768, 3072], P(('grp', 'fsdp'))
- grad_fc_out: float32 [3072, 768], P(('grp', 'fsdp'))
- grad_norm_gain: float32 [768, 4], P(('grp', 'fsdp'))
- grad_norm_bias: float32 [768, 4], P(('grp', 'fsdp'))
Inputs may be any that keep to these rules, and one draw needn't show every extreme that they name: `lengths`: each group of 16 sequences that one index of grp holds has one sequence of exactly 448 tokens; slots from a sequence's length on are padding.
All inputs are finite; a program needn't handle non-finite values.
Results may differ from a plain program's by a relative error of at most 0.02.
Values may be sent and summed in bfloat16 or wider, within the bound.
No kernel may reach another device: no remote copies, remote signals or barrier semaphores. Data moves between devices by JAX's collectives and lax.ppermute only.
A program may use at most 512 MiB of HBM per device.

v0:
```python
import functools

import jax
import jax.numpy as jnp
import numpy as np
from jax import lax
from jax.experimental import pallas as pl
from jax.experimental.pallas import tpu as pltpu
from jax.sharding import PartitionSpec as P

D = 768
FF = 3072
HEAD_DIM = 64
FRAMES = 1500
FRAME_SLOTS = 1536
PAIR = 2 * HEAD_DIM
PAIRS = D // PAIR
TILE = 128
ROWS = 256
KEY_CHUNK = 256
SOME = 3
FF_PARTS = FF // D

eps_norm = 1e-05
neg_big = -1e30
head_scale = 0.125
bf16 = jnp.bfloat16
f32 = jnp.float32
MIB = 1024 * 1024
COST = pl.CostEstimate(flops=1000000, bytes_accessed=1000000, transcendentals=0)

ONE_OUT = 3 * D
ONE_Q = 4 * D
ONE_NORM = 5 * D
ONE_COLS = 5 * D + 128
TWO_OUT = 2 * D


def nt(left, right):
    return lax.dot_general(left, right, (((1,), (1,)), ((), ())), preferred_element_type=f32)


def nn(left, right):
    return lax.dot_general(left, right, (((1,), (0,)), ((), ())), preferred_element_type=f32)


def normalize(stream):
    centered = stream - jnp.mean(stream, axis=-1, keepdims=True)
    scale = lax.rsqrt(jnp.mean(centered * centered, axis=-1, keepdims=True) + eps_norm)
    return centered * scale, scale


def norm_backward(normed, scale, gain, grad):
    scaled = grad * gain
    mean_scaled = jnp.mean(scaled, axis=-1, keepdims=True)
    mean_along = jnp.mean(scaled * normed, axis=-1, keepdims=True)
    return scale * (scaled - mean_scaled - normed * mean_along)


def col_sum(values):
    return jnp.sum(values, axis=0, keepdims=True)


def split_heads(block):
    lanes = lax.broadcasted_iota(jnp.int32, block.shape, 1)
    zero = jnp.zeros_like(block)
    return jnp.concatenate(
        [jnp.where(lanes < HEAD_DIM, block, zero), jnp.where(lanes < HEAD_DIM, zero, block)], axis=0
    )


def join_heads(stacked):
    width = stacked.shape[1] // 2
    return jnp.concatenate([stacked[:HEAD_DIM, :width], stacked[HEAD_DIM:, width:]], axis=0).T


def row_dots(left, right):
    prod = (left.astype(f32) * right.astype(f32)).T
    return jnp.concatenate([col_sum(prod[:HEAD_DIM]), col_sum(prod[HEAD_DIM:])], axis=1)


def seen(shape, row_start, seq_len):
    keys = lax.broadcasted_iota(jnp.int32, shape, 0)
    rows = row_start + lax.rem(lax.broadcasted_iota(jnp.int32, shape, 1), TILE)
    return (keys <= rows) & (keys < seq_len)


def each_tile(count, size, body):
    def step(i, carry):
        body(pl.ds(pl.multiple_of(i * size, size), size), i)
        return carry

    lax.fori_loop(0, count, step, 0)


def each_wide_tile(seq_len, body):
    count = pl.cdiv(seq_len, TILE)
    each_tile(count // 4, 4 * TILE, lambda rows, i: body(rows, 4 * TILE))
    for some in (2, 1):

        @pl.when(count // some % 2 == 1)
        def _():
            start = count // (2 * some) * (2 * some) * TILE
            body(pl.ds(pl.multiple_of(start, TILE), some * TILE), some * TILE)


def lane_block(index):
    return pl.ds(pl.multiple_of(index * PAIR, PAIR), PAIR)


def token_rows(ref, tile):
    count = ROWS // ref.shape[1]
    return ref[pl.ds(tile * count, count)].reshape(ROWS, D).astype(f32)


def clear(*refs):
    for ref in refs:
        ref[...] = jnp.zeros_like(ref)


scale_of_heads = functools.partial(jnp.asarray, head_scale, bf16)


def self_part_forward(
    len_ref, tok_ref, one_ref, norm_ref,
    qkv_ref, normed_one_ref, mix_ref, lse_ref, after_ref, normed_two_ref, q_two_ref,
    vt_ref,
):
    seq_len = len_ref[0]
    row_tiles = pl.cdiv(seq_len, ROWS)
    clear(normed_one_ref, mix_ref, lse_ref, normed_two_ref)

    def project(rows, i):
        normed, _ = normalize(token_rows(tok_ref, i))
        normed = (normed * norm_ref[0:1, :] + norm_ref[4:5, :]).astype(bf16)
        normed_one_ref[rows, :] = normed
        qkv_ref[rows, :] = nn(normed, one_ref[:, :ONE_OUT]).astype(bf16)

    each_tile(row_tiles, ROWS, project)

    def per_pair(pair, vt_ref, rows, tile):
        q_lanes, k_lanes, v_lanes = (lane_block(3 * pair + i) for i in range(3))
        size = (tile + 1) * TILE
        vt_ref[:, rows] = qkv_ref[rows, v_lanes].T
        queries = split_heads(qkv_ref[rows, q_lanes] * scale_of_heads())
        scores = nt(qkv_ref[:size, k_lanes], queries)
        scores = jnp.where(seen(scores.shape, tile * TILE, seq_len), scores, neg_big)
        peak = jnp.max(scores, axis=0, keepdims=True)
        probs = jnp.exp(scores - peak)
        total = col_sum(probs)
        mixed = nn(vt_ref[:, :size], probs.astype(bf16))
        mix_ref[rows, lane_block(pair)] = join_heads(mixed / total).astype(bf16)
        lse_ref[pair, tile : tile + 1, :] = peak + jnp.log(total)

    def some_pairs(step, carry):
        for tile in range(qkv_ref.shape[0] // TILE):

            @pl.when(tile * TILE < seq_len)
            def _():
                for i in range(SOME):
                    per_pair(step * SOME + i, vt_ref.at[i], slice(tile * TILE, (tile + 1) * TILE), tile)

        return carry

    lax.fori_loop(0, PAIRS // SOME, some_pairs, 0)

    def finish(rows, i):
        after = token_rows(tok_ref, i) + nn(mix_ref[rows, :], one_ref[:, ONE_OUT:ONE_Q])
        after_ref[rows, :] = after
        normed, _ = normalize(after)
        normed = (normed * norm_ref[1:2, :] + norm_ref[5:6, :]).astype(bf16)
        normed_two_ref[rows, :] = normed
        q_two_ref[rows, :] = nn(normed, one_ref[:, ONE_Q:ONE_NORM]).astype(bf16)

    each_tile(row_tiles, ROWS, finish)


PARTS = {"frames": 4, "tokens": 4, "first": 2, "second": 2, "all": 1}


def part_at(part):
    return {"frames": 0, "tokens": 3, "first": 0, "second": 1, "all": 0}[part]


def whole():
    return pl.BlockSpec(memory_space=pltpu.VMEM)


def in_smem():
    return pl.BlockSpec(memory_space=pltpu.SMEM)


def shape_of(*dims, dtype=bf16):
    return jax.ShapeDtypeStruct(dims, dtype)


def in_hbm(*dims, dtype=bf16):
    return pltpu.HBM(dims, dtype)


def run_self_forward(seq_len, arrived, part, one, norm_rows):
    blocks, size = arrived.shape[0], arrived.shape[1] // PARTS[part]
    at = part_at(part)
    rows = blocks * size
    fixed = lambda *dims: pl.BlockSpec(dims, lambda i: (0,) * len(dims), pipeline_mode=pl.Buffered(1))
    shapes = [
        in_hbm(rows, 3 * D),
        in_hbm(rows, D),
        in_hbm(rows, D),
        in_hbm(PAIRS, rows // TILE, 2 * TILE, dtype=f32),
        in_hbm(rows, D, dtype=f32),
        in_hbm(rows, D),
        in_hbm(rows, D),
    ]
    return pl.pallas_call(
        self_part_forward,
        name="self_part_forward",
        grid=(1,),
        in_specs=[
            in_smem(),
            pl.BlockSpec((blocks, size, D), lambda i: (0, at, 0), pipeline_mode=pl.Buffered(1)),
            fixed(*one.shape),
            fixed(8, D),
        ],
        out_specs=[fixed(*s.shape) for s in shapes],
        out_shape=shapes,
        scratch_shapes=[pltpu.VMEM((SOME, PAIR, rows), bf16)],
        compiler_params=pltpu.CompilerParams(vmem_limit_bytes=36 * MIB),
        cost_estimate=COST,
    )(seq_len, arrived, one, norm_rows)


def cross_forward_kernel(len_ref, frm_ref, w_ref, q_ref, out_ref, lse_ref, kv_ref, vt_ref, s_ref):
    slots = kv_ref.shape[0]
    clear(out_ref, lse_ref)
    kv_ref[...] = nn(frm_ref[...].reshape(slots, D), w_ref[...]).astype(bf16)
    vt_ref[...] = kv_ref[:, PAIR:].T
    spans = [(k, min(KEY_CHUNK, slots - k)) for k in range(0, slots, KEY_CHUNK)]

    def per_tile(rows, width):
        queries = split_heads(q_ref[rows, :] * scale_of_heads())
        peak = jnp.full((1, 2 * width), neg_big, f32)
        for start, size in spans:
            scores = nt(kv_ref[start : start + size, :PAIR], queries)
            if start + size > FRAMES:
                keys = start + lax.broadcasted_iota(jnp.int32, scores.shape, 0)
                scores = jnp.where(keys < FRAMES, scores, neg_big)
            s_ref[start : start + size, : 2 * width] = scores
            peak = jnp.maximum(peak, jnp.max(scores, axis=0, keepdims=True))
        total = jnp.zeros((1, 2 * width), f32)
        mixed = jnp.zeros((PAIR, 2 * width), f32)
        for start, size in spans:
            probs = jnp.exp(s_ref[start : start + size, : 2 * width] - peak)
            total = total + col_sum(probs)
            mixed = mixed + nn(vt_ref[:, start : start + size], probs.astype(bf16))
        out_ref[rows, :] = join_heads(mixed / total).astype(bf16)
        log_sum = peak + jnp.log(total)
        lse_ref[0, 0:1, rows] = log_sum[:, :width]
        lse_ref[0, 1:2, rows] = log_sum[:, width:]

    each_wide_tile(len_ref[0], per_tile)


def frame_rows(arrived):
    return FRAME_SLOTS // arrived.shape[0]


def run_cross_forward(seq_len, arrived, two, q_two):
    blocks, size = arrived.shape[0], frame_rows(arrived)
    rows, slots = q_two.shape[0], blocks * size
    return pl.pallas_call(
        cross_forward_kernel,
        name="cross_forward",
        grid=(PAIRS,),
        in_specs=[
            in_smem(),
            pl.BlockSpec((blocks, size, D), lambda h: (0, 0, 0), pipeline_mode=pl.Buffered(1)),
            pl.BlockSpec((D, 2 * PAIR), lambda h: (0, h)),
            pl.BlockSpec((rows, PAIR), lambda h: (0, h)),
        ],
        out_specs=[
            pl.BlockSpec((rows, PAIR), lambda h: (0, h)),
            pl.BlockSpec((1, 2, rows), lambda h: (h, 0, 0)),
            pl.BlockSpec((slots, 2 * PAIR), lambda h: (0, h)),
        ],
        out_shape=[
            in_hbm(rows, D),
            in_hbm(PAIRS, 2, rows, dtype=f32),
            in_hbm(slots, 2 * D),
        ],
        scratch_shapes=[pltpu.VMEM((PAIR, slots), bf16), pltpu.VMEM((slots, 8 * TILE), f32)],
        compiler_params=pltpu.CompilerParams(vmem_limit_bytes=24 * MIB),
        cost_estimate=COST,
    )(seq_len, arrived, two, q_two)


def cross_backward_kernel(
    len_ref, q_ref, kv_ref, mix_ref, grad_ref, lse_ref, w_ref, _,
    dq_ref, dkv_ref, dfrm_ref,
    kt_ref, dk_ref, dv_ref, acc_ref,
):
    slots = kv_ref.shape[0]
    pair = pl.program_id(0)
    kt_ref[...] = kv_ref[:, :PAIR].T
    clear(dq_ref, dk_ref, dv_ref)
    spans = [(k, min(KEY_CHUNK, slots - k)) for k in range(0, slots, KEY_CHUNK)]

    def per_tile(rows, width):
        queries = split_heads(q_ref[rows, :] * scale_of_heads())
        grads = split_heads(grad_ref[rows, :])
        inner = row_dots(mix_ref[rows, :], grad_ref[rows, :])
        lse = jnp.concatenate([lse_ref[0, 0:1, rows], lse_ref[0, 1:2, rows]], axis=1)
        dq = jnp.zeros((PAIR, 2 * width), f32)
        for start, size in spans:
            span = slice(start, start + size)
            probs = jnp.exp(nt(kv_ref[span, :PAIR], queries) - lse)
            if start + size > FRAMES:
                keys = start + lax.broadcasted_iota(jnp.int32, probs.shape, 0)
                probs = jnp.where(keys < FRAMES, probs, 0.0)
            dscores = (probs * (nt(kv_ref[span, PAIR:], grads) - inner)).astype(bf16)
            dv_ref[span, :] += nn(probs.astype(bf16), grads)
            dk_ref[span, :] += nn(dscores, queries)
            dq = dq + nn(kt_ref[:, span], dscores)
        dq_ref[rows, :] = join_heads(dq).astype(bf16) * scale_of_heads()

    each_wide_tile(len_ref[0], per_tile)
    dkv_ref[:, :PAIR] = dk_ref[...].astype(bf16)
    dkv_ref[:, PAIR:] = dv_ref[...].astype(bf16)
    part = nt(dkv_ref[...], w_ref[...])

    @pl.when(pair == 0)
    def _():
        acc_ref[...] = part

    @pl.when((pair > 0) & (pair < PAIRS - 1))
    def _():
        acc_ref[...] += part

    @pl.when(pair == PAIRS - 1)
    def _():
        dfrm_ref[...] = (acc_ref[...] + part).astype(bf16).reshape(dfrm_ref.shape)


def run_cross_backward(seq_len, q_two, kv, mix, grad_mix, lse, two, leaving):
    rows, slots, blocks = q_two.shape[0], kv.shape[0], leaving.shape[0]
    row_spec = pl.BlockSpec((rows, PAIR), lambda h: (0, h))
    kv_spec = pl.BlockSpec((slots, 2 * PAIR), lambda h: (0, h))
    return pl.pallas_call(
        cross_backward_kernel,
        name="cross_backward",
        grid=(PAIRS,),
        in_specs=[
            in_smem(),
            row_spec,
            kv_spec,
            row_spec,
            row_spec,
            pl.BlockSpec((1, 2, rows), lambda h: (h, 0, 0)),
            pl.BlockSpec((D, 2 * PAIR), lambda h: (0, h)),
            pl.BlockSpec(memory_space=pl.ANY),
        ],
        out_specs=[
            row_spec,
            kv_spec,
            pl.BlockSpec((blocks, slots // blocks, D), lambda h: (0, 0, 0), pipeline_mode=pl.Buffered(1)),
        ],
        out_shape=[in_hbm(rows, D), in_hbm(slots, 2 * D), in_hbm(*leaving.shape)],
        input_output_aliases={7: 2},
        scratch_shapes=[
            pltpu.VMEM((PAIR, slots), bf16),
            pltpu.VMEM((slots, PAIR), f32),
            pltpu.VMEM((slots, PAIR), f32),
            pltpu.VMEM((slots, D), f32),
        ],
        compiler_params=pltpu.CompilerParams(vmem_limit_bytes=36 * MIB),
        cost_estimate=COST,
    )(seq_len, q_two, kv, mix, grad_mix, lse, two, leaving)


def middle_kernel(
    len_ref, mix_ref, after_ref, cot_ref, two_ref, fc_ref, norm_ref,
    out_ref, normed_ref, hidden_ref, grad_pre_ref, branch_three_ref, branch_two_ref,
    grad_cross_ref, grad_mix_ref, norm_grad_ref,
    slope_ref,
):
    seq_len = len_ref[0]
    step = pl.program_id(0)
    parts = [(slice(k, k + D), slice(FF + k, FF + k + D)) for k in range(0, FF, D)]

    @pl.when(step == 0)
    def _():
        clear(norm_grad_ref)

    @pl.when(step * ROWS >= seq_len)
    def _():
        clear(out_ref)

    @pl.when(step * ROWS < seq_len)
    def _():
        w_out = two_ref[:, TWO_OUT:]
        after_cross = after_ref[...] + nn(mix_ref[...], w_out)
        n_three, scale_three = normalize(after_cross)
        normed = (n_three * norm_ref[2:3, :] + norm_ref[6:7, :]).astype(bf16)
        normed_ref[...] = normed
        mlp = jnp.zeros((ROWS, D), f32)
        for span, rows_out in parts:
            pre = nn(normed, fc_ref[:, span])
            below = 0.5 * (1.0 + lax.erf(pre * np.float32(np.sqrt(0.5))))
            density = jnp.exp(-0.5 * pre * pre) * np.float32(1.0 / np.sqrt(2.0 * np.pi))
            slope_ref[:, span] = below + pre * density
            hidden = (pre * below).astype(bf16)
            hidden_ref[:, span] = hidden
            mlp = mlp + nn(hidden, fc_ref[:, rows_out])
        n_four, scale_four = normalize(after_cross + mlp)
        row_ids = step * ROWS + lax.broadcasted_iota(jnp.int32, (ROWS, 1), 0)
        valid = (row_ids < seq_len).astype(f32)
        output = ((n_four * norm_ref[3:4, :] + norm_ref[7:8, :]) * valid).astype(bf16)
        out_ref[...] = output.reshape(out_ref.shape)

        grad = cot_ref[...].reshape(ROWS, D).astype(f32) * valid
        norm_grad_ref[1:2, :] += col_sum(grad * n_four)
        norm_grad_ref[3:4, :] += col_sum(grad)
        grad_mlp = norm_backward(n_four, scale_four, norm_ref[3:4, :], grad)
        branch_three = grad_mlp.astype(bf16)
        branch_three_ref[...] = branch_three
        back = jnp.zeros((ROWS, D), f32)
        for span, rows_out in parts:
            grad_pre = (nt(branch_three, fc_ref[:, rows_out]) * slope_ref[:, span]).astype(bf16)
            grad_pre_ref[:, span] = grad_pre
            back = back + nt(grad_pre, fc_ref[:, span])
        norm_grad_ref[0:1, :] += col_sum(back * n_three)
        norm_grad_ref[2:3, :] += col_sum(back)
        grad_cross = grad_mlp + norm_backward(n_three, scale_three, norm_ref[2:3, :], back)
        grad_cross_ref[...] = grad_cross
        branch_two = grad_cross.astype(bf16)
        branch_two_ref[...] = branch_two
        grad_mix_ref[...] = nt(branch_two, w_out).astype(bf16)


def run_middle(seq_len, mix, after, arrived, part, two, fc, norm_rows):
    rows, blocks = mix.shape[0], arrived.shape[0]
    size = rows // blocks
    at = part_at(part)
    count = ROWS // size
    last = lambda i, n: jnp.minimum(i, (n[0] - 1) // ROWS)
    row_spec = pl.BlockSpec((ROWS, D), lambda i, n: (last(i, n), 0))
    wide_spec = pl.BlockSpec((ROWS, FF), lambda i, n: (last(i, n), 0))

    def fixed(*dims):
        return pl.BlockSpec(dims, lambda i, n: (0, 0), pipeline_mode=pl.Buffered(1))

    return pl.pallas_call(
        middle_kernel,
        name="mlp_and_back",
        grid_spec=pltpu.PrefetchScalarGridSpec(
            num_scalar_prefetch=1,
            grid=(rows // ROWS,),
            in_specs=[
                row_spec, row_spec, pl.BlockSpec((count, size, D), lambda i, n: (last(i, n), at, 0)),
                fixed(D, 3 * D), fixed(D, 2 * FF), fixed(8, D),
            ],
            out_specs=[pl.BlockSpec((count, size, D), lambda i, n: (i, 3, 0)), row_spec, wide_spec, wide_spec, row_spec, row_spec, row_spec, row_spec,
                   pl.BlockSpec((8, D), lambda i, n: (0, 0))],
            scratch_shapes=[pltpu.VMEM((ROWS, FF), f32)],
        ),
        out_shape=[
            in_hbm(blocks, 4 * size, D), in_hbm(rows, D), in_hbm(rows, FF), in_hbm(rows, FF),
            in_hbm(rows, D), in_hbm(rows, D), in_hbm(rows, D, dtype=f32), in_hbm(rows, D),
            in_hbm(8, D, dtype=f32),
        ],
        compiler_params=pltpu.CompilerParams(vmem_limit_bytes=48 * MIB),
        cost_estimate=COST,
    )(seq_len, mix, after, arrived, two, fc, norm_rows)


def self_part_backward(
    len_ref, dq_ref, grad_cross_ref, after_ref, qkv_ref, mix_ref, lse_ref, tok_ref, one_ref, norm_ref, _,
    branch_ref, dqkv_ref, grad_tok_ref, norm_grad_ref,
    attn_ref, grad_mix_ref, kt_ref, dk_ref, dv_ref,
):
    seq_len = len_ref[0]
    row_tiles = pl.cdiv(seq_len, ROWS)
    clear(branch_ref, dqkv_ref, grad_tok_ref, norm_grad_ref)

    def enter(rows, _):
        normed, scale = normalize(after_ref[rows, :])
        grad = nt(dq_ref[rows, :], one_ref[:, ONE_Q:ONE_NORM])
        norm_grad_ref[1:2, :] += col_sum(grad * normed)
        norm_grad_ref[3:4, :] += col_sum(grad)
        attn = grad_cross_ref[rows, :] + norm_backward(normed, scale, norm_ref[1:2, :], grad)
        attn_ref[rows, :] = attn
        branch = attn.astype(bf16)
        branch_ref[rows, :] = branch
        grad_mix_ref[rows, :] = nt(branch, one_ref[:, ONE_OUT:ONE_Q]).astype(bf16)

    each_tile(row_tiles, ROWS, enter)

    def per_pair(pair, kt_ref, dk_ref, dv_ref, rows, tile):
        q_lanes, k_lanes, v_lanes = (lane_block(3 * pair + i) for i in range(3))
        size = (tile + 1) * TILE
        kt_ref[:, rows] = qkv_ref[rows, k_lanes].T
        queries = split_heads(qkv_ref[rows, q_lanes] * scale_of_heads())
        grad_mix = grad_mix_ref[rows, lane_block(pair)]
        grads = split_heads(grad_mix)
        inner = row_dots(mix_ref[rows, lane_block(pair)], grad_mix)
        scores = nt(qkv_ref[:size, k_lanes], queries)
        scores = jnp.where(seen(scores.shape, tile * TILE, seq_len), scores, neg_big)
        probs = jnp.exp(scores - lse_ref[pair, tile : tile + 1, :])
        dscores = (probs * (nt(qkv_ref[:size, v_lanes], grads) - inner)).astype(bf16)
        dv_ref[:size, :] += nn(probs.astype(bf16), grads)
        dk_ref[:size, :] += nn(dscores, queries)
        dq = nn(kt_ref[:, :size], dscores)
        dqkv_ref[rows, q_lanes] = join_heads(dq).astype(bf16) * scale_of_heads()

    def some_pairs(step, carry):
        clear(dk_ref, dv_ref)
        for tile in range(qkv_ref.shape[0] // TILE):

            @pl.when(tile * TILE < seq_len)
            def _():
                for i in range(SOME):
                    rows = slice(tile * TILE, (tile + 1) * TILE)
                    per_pair(step * SOME + i, kt_ref.at[i], dk_ref.at[i], dv_ref.at[i], rows, tile)

        for i in range(SOME):
            pair = step * SOME + i
            dqkv_ref[:, lane_block(3 * pair + 1)] = dk_ref[i].astype(bf16)
            dqkv_ref[:, lane_block(3 * pair + 2)] = dv_ref[i].astype(bf16)
        return carry

    lax.fori_loop(0, PAIRS // SOME, some_pairs, 0)

    def leave(rows, i):
        normed, scale = normalize(token_rows(tok_ref, i))
        grad = nt(dqkv_ref[rows, :], one_ref[:, :ONE_OUT])
        norm_grad_ref[0:1, :] += col_sum(grad * normed)
        norm_grad_ref[2:3, :] += col_sum(grad)
        total = attn_ref[rows, :] + norm_backward(normed, scale, norm_ref[0:1, :], grad)
        count = ROWS // grad_tok_ref.shape[1]
        grad_tok_ref[pl.ds(i * count, count)] = total.astype(bf16).reshape(count, -1, D)

    each_tile(row_tiles, ROWS, leave)


def run_self_backward(seq_len, dq, grad_cross, after, qkv, mix, lse, arrived, part, one, norm_rows, leaving, slot):
    blocks, size = arrived.shape[0], arrived.shape[1] // PARTS[part]
    at = part_at(part)
    rows = blocks * size
    fixed = lambda *dims: pl.BlockSpec(dims, lambda i: (0,) * len(dims), pipeline_mode=pl.Buffered(1))
    spec = lambda block: pl.BlockSpec(
        (blocks, size, D), lambda i: (0, block, 0), pipeline_mode=pl.Buffered(1)
    )
    before = [] if leaving is None else [leaving]
    body = self_part_backward
    if leaving is None:
        body = lambda *refs: self_part_backward(*refs[:10], None, *refs[10:])
    return pl.pallas_call(
        body,
        name="self_part_backward",
        grid=(1,),
        in_specs=[in_smem()]
        + [fixed(*a.shape) for a in (dq, grad_cross, after, qkv, mix, lse)]
        + [spec(at), fixed(*one.shape), fixed(8, D)]
        + [anywhere()] * len(before),
        out_specs=[fixed(rows, D), fixed(rows, 3 * D), spec(slot), fixed(8, D)],
        out_shape=[
            in_hbm(rows, D),
            in_hbm(rows, 3 * D),
            in_hbm(blocks, 2 * size, D),
            in_hbm(8, D, dtype=f32),
        ],
        input_output_aliases={10: 2} if before else {},
        scratch_shapes=[
            pltpu.VMEM((rows, D), f32),
            pltpu.VMEM((rows, D), bf16),
            pltpu.VMEM((SOME, PAIR, rows), bf16),
            pltpu.VMEM((SOME, rows, PAIR), f32),
            pltpu.VMEM((SOME, rows, PAIR), f32),
        ],
        compiler_params=pltpu.CompilerParams(vmem_limit_bytes=40 * MIB),
        cost_estimate=COST,
    )(seq_len, dq, grad_cross, after, qkv, mix, lse, arrived, one, norm_rows, *before)


def anywhere():
    return pl.BlockSpec(memory_space=pl.ANY)


def copy_kernel(plan, n_in, n_out, scalar_ref, *refs):
    ins, outs, sem = refs[:n_in], refs[n_in : n_in + n_out], refs[-1]
    for which, src, dst in plan(scalar_ref, ins, outs):
        pltpu.make_async_copy(src, dst, sem.at[which]).start()
    for which, out in enumerate(outs):
        pltpu.make_async_copy(out, out, sem.at[which]).wait()


def run_copies(name, plan, scalars, ins, out_shapes, stage="in"):
    vmem = pl.BlockSpec(memory_space=pltpu.VMEM)
    return pl.pallas_call(
        functools.partial(copy_kernel, plan, len(ins), len(out_shapes)),
        name=name,
        in_specs=[in_smem()] + [vmem if stage == "in" else pl.BlockSpec(memory_space=pltpu.HBM)] * len(ins),
        out_specs=[vmem if stage == "out" else anywhere()] * len(out_shapes),
        out_shape=out_shapes,
        scratch_shapes=[pltpu.SemaphoreType.DMA((len(out_shapes),))],
        compiler_params=pltpu.CompilerParams(vmem_limit_bytes=16 * MIB),
        cost_estimate=pl.CostEstimate(flops=0, bytes_accessed=1000, transcendentals=0),
    )(scalars, *ins)


def device_bits():
    return [
        (axis, b)
        for axis in ("grp", "fsdp")
        for b in reversed(range(lax.axis_size(axis).bit_length() - 1))
    ]


def swap(array, axis, b):
    return lax.ppermute(array, axis, [(i, i ^ (1 << b)) for i in range(lax.axis_size(axis))])


def bit_mask(axis, b):
    return (1 << b) if axis == "fsdp" else lax.axis_size("fsdp") << b


def my_bit(axis, b):
    return (lax.axis_index(axis) >> b) & 1


class Gather:
    def __init__(self, name, shard, me, outs, pieces):
        self.name = name
        bits = device_bits()
        self.left = [p for p in bits if p[0] == "fsdp"] + [p for p in bits if p[0] == "grp"]
        self.masks = [0]
        self.value = shard[None]
        self.me = me
        self.outs = outs
        self.pieces = pieces
        self.got = None

    def send(self):
        self.got = swap(self.value, *self.left[0])

    def take(self):
        mask = bit_mask(*self.left.pop(0))
        masks = self.masks
        self.masks = masks + [mask ^ m for m in masks]
        k = len(masks)
        if self.left:

            def plan(_, ins, outs):
                return [(0, ins[0], outs[0].at[:k]), (0, ins[1], outs[0].at[k:])]

            shape = (2 * k,) + self.value.shape[1:]
            (self.value,) = run_copies(
                self.name + "_join", plan, self.me, [self.value, self.got], [in_hbm(*shape)]
            )
            return self.value

        def plan(me_ref, ins, outs):
            me = me_ref[0]
            return [
                (which, src, dst)
                for i in range(k)
                for half, src_ref in ((0, ins[0]), (k, ins[1]))
                for which, src, dst in self.pieces(src_ref.at[i], outs, me ^ self.masks[half + i])
            ]

        self.value = run_copies(
            self.name + "_order", plan, self.me, [self.value, self.got], self.outs
        )
        return self.value

    def step(self):
        self.send()
        return self.take()


def pack_shards(me, self_in, self_out, cross_q, norms, cross_kv, cross_out):
    rows = self_in.shape[0]

    def plan(_, ins, outs):
        w_in, w_out, w_q, w_norm, w_kv, w_cross = ins
        one, two = outs
        copies = []
        for pair in range(PAIRS):
            for o, w, parts in ((0, w_in, 3), (1, w_kv, 2)):
                for part in range(parts):
                    src = w.at[:, part * D + pair * PAIR : part * D + (pair + 1) * PAIR]
                    at = (parts * pair + part) * PAIR
                    copies.append((o, src, outs[o].at[:, at : at + PAIR]))
        copies.append((0, w_out, one.at[:, ONE_OUT:ONE_Q]))
        copies.append((0, w_q, one.at[:, ONE_Q:ONE_NORM]))
        copies.append((0, w_norm, one.at[:, ONE_NORM:]))
        copies.append((1, w_cross, two.at[:, TWO_OUT:]))
        return copies

    ins = [self_in, self_out, cross_q, norms, cross_kv, cross_out]
    shapes = [in_hbm(rows, ONE_COLS), in_hbm(rows, 3 * D)]
    return run_copies("pack_shards", plan, me, ins, shapes, "out")


def gather_rows(shard):
    return lax.all_gather(shard, ("grp", "fsdp"), axis=0, tiled=True)


def grad_kernel(
    full, len0_ref, len1_ref, bit_ref, left0_ref, right0_ref, left1_ref, right1_ref, *refs
):
    keep_ref, send_ref, flip_ref, acc_ref = refs[-4:]
    half, count = keep_ref.shape[1], right0_ref.shape[0]
    sides = (
        (len0_ref[0], left0_ref, right0_ref, 0),
        (len1_ref[0], left1_ref, right1_ref, count),
    )
    tiles = [slice(k, k + ROWS) for k in range(0, count, ROWS)]

    @pl.when(pl.program_id(0) == 0)
    def _():
        for seq_len, left_ref, _, at in sides:
            for tile in tiles:

                @pl.when(jnp.logical_or(full or tile.start == 0, tile.start < seq_len))
                def _():
                    if len(left_ref.shape) == 3:
                        size = left_ref.shape[1]
                        left = left_ref[tile.start // size : (tile.stop + size - 1) // size]
                        skip = tile.start % size
                        left = left.reshape(-1, D)[skip : skip + ROWS]
                    else:
                        left = left_ref[tile, :]
                    flip_ref[:, at + tile.start : at + tile.stop] = left.T

    if full:
        acc_ref[...] = nn(flip_ref[:, :count], right0_ref[...]) + nn(
            flip_ref[:, count:], right1_ref[...]
        )
    else:
        acc_ref[...] = nn(flip_ref[:, :ROWS], right0_ref[:ROWS, :]) + nn(
            flip_ref[:, count : count + ROWS], right1_ref[:ROWS, :]
        )
        for seq_len, _, right_ref, at in sides:
            for tile in tiles[1:]:

                @pl.when(tile.start < seq_len)
                def _():
                    acc_ref[...] += nn(flip_ref[:, at + tile.start : at + tile.stop], right_ref[tile, :])

    for i in range(keep_ref.shape[0]):
        for out_ref, bit in ((keep_ref, bit_ref[0]), (send_ref, 1 - bit_ref[0])):
            at = pl.multiple_of((2 * i + bit) * half, half)
            out_ref[i] = acc_ref[pl.ds(at, half), :].astype(bf16)


def fc_grad_kernel(
    len0_ref, len1_ref, normed0_ref, pre0_ref, hid0_ref, branch0_ref, normed1_ref, pre1_ref, hid1_ref, branch1_ref,
    out_ref, flip_ref, acc_ref,
):
    step = pl.program_id(0)
    count = normed0_ref.shape[0]
    tiles = [slice(k, k + ROWS) for k in range(0, count, ROWS)]
    sides = (
        (len0_ref[0], normed0_ref, pre0_ref, hid0_ref, branch0_ref, 0),
        (len1_ref[0], normed1_ref, pre1_ref, hid1_ref, branch1_ref, count),
    )

    def flip(pick):
        for side in sides:
            for tile in tiles:

                @pl.when(jnp.logical_or(tile.start == 0, tile.start < side[0]))
                def _():
                    flip_ref[:, side[5] + tile.start : side[5] + tile.stop] = side[pick][tile, :].T

    def multiply(pick):
        acc_ref[...] = nn(flip_ref[:, :ROWS], sides[0][pick][:ROWS, :]) + nn(
            flip_ref[:, count : count + ROWS], sides[1][pick][:ROWS, :]
        )
        for side in sides:
            for tile in tiles[1:]:

                @pl.when(tile.start < side[0])
                def _():
                    at = side[5]
                    acc_ref[...] += nn(flip_ref[:, at + tile.start : at + tile.stop], side[pick][tile, :])

        out_ref[...] = acc_ref[...].astype(bf16)

    @pl.when(step == 0)
    def _():
        flip(1)

    @pl.when(step < FF_PARTS)
    def _():
        multiply(2)

    @pl.when(step >= FF_PARTS)
    def _():
        flip(3)
        multiply(4)


def norm_grad_kernel(bit_ref, norm_ref, _, __, keep_ref, send_ref, flip_ref):
    flip_ref[...] = jnp.concatenate([norm_ref[...], jnp.zeros((PAIR - 8, D), f32)], axis=0).T
    size = keep_ref.shape[1]
    for i in range(keep_ref.shape[0]):
        for out_ref, bit in ((keep_ref, bit_ref[0]), (send_ref, 1 - bit_ref[0])):
            at = pl.multiple_of((2 * i + bit) * size, size)
            out_ref[i] = flip_ref[pl.ds(at, size), :].astype(bf16)


def put_norm_grad(norm_sum, halves):
    count, size, cols = halves[0].shape
    spec = pl.BlockSpec((count, size, PAIR), lambda i: (0, 0, cols // PAIR - 1))
    return pl.pallas_call(
        norm_grad_kernel,
        name="put_norm_grad",
        grid=(1,),
        in_specs=[in_smem(), pl.BlockSpec((8, D), lambda i: (0, 0)), anywhere(), anywhere()],
        out_specs=[spec, spec],
        out_shape=[in_hbm(*h.shape) for h in halves],
        input_output_aliases={2: 0, 3: 1},
        scratch_shapes=[pltpu.VMEM((D, PAIR), f32)],
        compiler_params=pltpu.CompilerParams(vmem_limit_bytes=8 * MIB),
        cost_estimate=COST,
    )(my_bit("grp", 0).reshape(1), norm_sum, *halves)


def run_fc_grad(lens, side0, side1):
    count = side0[0].shape[0]
    whole_spec = pl.BlockSpec((count, D), lambda i: (0, 0), pipeline_mode=pl.Buffered(1))
    pre_spec = pl.BlockSpec((count, D), lambda i: (0, jnp.minimum(i, FF_PARTS - 1)))
    hid_spec = pl.BlockSpec((count, D), lambda i: (0, jnp.maximum(i - FF_PARTS, 0)))
    return pl.pallas_call(
        fc_grad_kernel,
        name="grad_fc",
        grid=(2 * FF_PARTS,),
        in_specs=[in_smem()] * 2 + [whole_spec, pre_spec, hid_spec, whole_spec] * 2,
        out_specs=pl.BlockSpec((D, D), lambda i: (0, i)),
        out_shape=in_hbm(D, 2 * FF),
        scratch_shapes=[pltpu.VMEM((D, 2 * count), bf16), pltpu.VMEM((D, D), f32)],
        compiler_params=pltpu.CompilerParams(vmem_limit_bytes=32 * MIB),
        cost_estimate=COST,
    )(*lens, *side0, *side1)


def run_grad(name, lens, pairs, cols, at, before=(), full=False):
    (left0, right0), (left1, right1) = pairs
    count, wide = right0.shape
    tall = D
    n_grp = lax.axis_size("grp")
    def left_spec(left):
        if left.ndim == 3:
            block = (left.shape[0], frame_rows(left), D)
            return pl.BlockSpec(block, lambda n: (0, 0, 0), pipeline_mode=pl.Buffered(1))
        return pl.BlockSpec((count, tall), lambda n: (0, 0), pipeline_mode=pl.Buffered(1))

    right_spec = pl.BlockSpec((count, D), lambda n: (0, n))
    out_spec = pl.BlockSpec((n_grp // 2, tall // n_grp, D), lambda n: (0, 0, n + at))
    shape = in_hbm(n_grp // 2, tall // n_grp, cols)
    bit = my_bit("grp", 0).reshape(1)
    return pl.pallas_call(
        functools.partial(grad_kernel, full),
        name=name,
        grid=(wide // D,),
        in_specs=[in_smem()] * 3
        + [left_spec(left0), right_spec, left_spec(left1), right_spec]
        + [anywhere()] * len(before),
        out_specs=[out_spec, out_spec],
        out_shape=[shape, shape],
        input_output_aliases={7: 0, 8: 1} if before else {},
        scratch_shapes=[pltpu.VMEM((tall, 2 * count), bf16), pltpu.VMEM((tall, D), f32)],
        compiler_params=pltpu.CompilerParams(vmem_limit_bytes=48 * MIB),
        cost_estimate=COST,
    )(*lens, bit, left0, right0, left1, right1, *before)


def add_split_kernel(me_ref, kept_ref, got_ref, keep_ref, send_ref):
    for out_ref, half in ((keep_ref, me_ref[0]), (send_ref, 1 - me_ref[0])):
        total = kept_ref[0, half].astype(f32) + got_ref[0, half].astype(f32)
        out_ref[0] = total.astype(out_ref.dtype)


def add_kernel(kept_ref, got_ref, out_ref):
    out_ref[...] = kept_ref[...].astype(f32) + got_ref[...].astype(f32)


class Scatter:
    def __init__(self, name, keep, send):
        self.name = name
        self.held = device_bits()
        self.order = [p for p in reversed(self.held) if p[0] == "grp"]
        self.order += [p for p in reversed(self.held) if p[0] == "fsdp"]
        self.split()
        blocks = 1 << len(self.held)
        self.keep, self.send = (a.reshape(blocks, -1, a.shape[-1]) for a in (keep, send))
        self.block = self.keep.shape[1:]

    def split(self):
        self.bit = self.order.pop(0)
        dim = self.held.index(self.bit)
        self.held.remove(self.bit)
        return 1 << dim, 1 << (len(self.held) - dim)

    def move(self):
        self.got = swap(self.send, *self.bit)

    def step(self):
        self.move()
        return self.take()

    def take(self):
        got = self.got
        if not self.order:
            spec = pl.BlockSpec((1,) + self.block, lambda i: (0, 0, 0))
            return pl.pallas_call(
                add_kernel,
                name=self.name + "_sum",
                grid=(1,),
                in_specs=[spec, spec],
                out_specs=spec,
                out_shape=shape_of(1, *self.block, dtype=f32),
                compiler_params=pltpu.CompilerParams(vmem_limit_bytes=8 * MIB),
                cost_estimate=COST,
            )(self.keep, got).reshape(self.block)
        before, after = self.split()
        half = self.keep.shape[0] // 2
        view = (before, 2, after) + self.block
        some = min(after, 4)
        in_spec = pl.BlockSpec((1, 2, some) + self.block, lambda i, j, _: (i, 0, j, 0, 0))
        out_spec = pl.BlockSpec((1, some) + self.block, lambda i, j, _: (i, j, 0, 0))
        shape = shape_of(before, after, *self.block, dtype=self.keep.dtype)
        keep, send = pl.pallas_call(
            add_split_kernel,
            name=self.name + "_add",
            grid_spec=pltpu.PrefetchScalarGridSpec(
                num_scalar_prefetch=1,
                grid=(before, after // some),
                in_specs=[in_spec, in_spec],
                out_specs=[out_spec, out_spec],
            ),
            out_shape=[shape, shape],
            compiler_params=pltpu.CompilerParams(vmem_limit_bytes=16 * MIB),
            cost_estimate=COST,
        )(my_bit(*self.bit).reshape(1), self.keep.reshape(view), got.reshape(view))
        self.keep, self.send = (a.reshape((half,) + self.block) for a in (keep, send))

    def finish(self):
        while True:
            done = self.take()
            if done is not None:
                return done
            self.move()


def fence(*values):
    return lax.optimization_barrier(values)


def by_part(weight, parts):
    rows = weight.shape[0]
    return weight.reshape(rows, PAIRS, parts, PAIR).swapaxes(1, 2).reshape(rows, parts * D)


def rows_of(array):
    return array.reshape(-1, array.shape[-1])


def exchange(array):
    return lax.all_to_all(array, "fsdp", split_axis=0, concat_axis=0, tiled=True)


def shards(
    tokens,
    frames,
    lengths,
    cotangent,
    self_in,
    self_out,
    cross_q,
    cross_kv,
    cross_out,
    fc_in,
    fc_out,
    norm_gain,
    norm_bias,
):
    fsdp_count = lax.axis_size("fsdp")
    n_all = lax.axis_size("grp") * fsdp_count
    group_seqs, size = tokens.shape[:2]
    seq_ids = jnp.arange(group_seqs, dtype=jnp.int32)
    rank_order = jnp.argsort(-(lengths * group_seqs + (group_seqs - 1 - seq_ids)))
    sender = jnp.concatenate([rank_order[:fsdp_count], rank_order[fsdp_count:][::-1]])
    device = lax.axis_index("fsdp")
    len0, len1 = (
        lax.dynamic_slice_in_dim(lengths[sender], s * fsdp_count + device, 1) for s in range(2)
    )
    rows = self_in.shape[0]
    me = (lax.axis_index("grp") * fsdp_count + device).reshape(1)

    def pick(name, *parts):
        total = sum(array.shape[1] for array, _ in parts)

        def plan(seq_ref, ins, outs):
            copies, at = [], 0
            for src, (array, slot) in zip(ins, parts):
                span = slice(at, at + array.shape[1])
                at += array.shape[1]
                for j in range(fsdp_count):
                    seq = seq_ref[slot * fsdp_count + j]
                    copies.append((0, src.at[seq], outs[0].at[j, span]))
            return copies

        shape = in_hbm(fsdp_count, total, D)
        return run_copies(name, plan, sender, [array for array, _ in parts], [shape], "out")[0]

    def put_back(name, *parts):
        ins = []
        for first, _, second, _ in parts:
            ins += [a for a in (first, second) if not any(a is b for b in ins)]
        where = [[next(i for i, a in enumerate(ins) if a is p[k]) for k in (0, 2)] for p in parts]

        def plan(seq_ref, in_refs, outs):
            return [
                (o, in_refs[where[o][slot]].at[j, part[2 * slot + 1]], outs[o].at[seq_ref[slot * fsdp_count + j]])
                for o, part in enumerate(parts)
                for slot in range(2)
                for j in range(fsdp_count)
            ]

        shapes = [in_hbm(group_seqs, p[1].stop - p[1].start, D) for p in parts]
        return run_copies(name, plan, sender, ins, shapes)

    norms = jnp.pad(jnp.concatenate([norm_gain, norm_bias], axis=1), ((0, 0), (0, 120)))
    shard_one, shard_two = pack_shards(me, self_in, self_out, cross_q, norms, cross_kv, cross_out)
    w_two = gather_rows(shard_two)
    one = Gather(
        "one", shard_one, me, [in_hbm(n_all, rows, ONE_COLS)],
        lambda src, outs, b: [(0, src, outs[0].at[b])],
    )

    pick_t = pick("pick_tokens", (tokens, 0), (tokens, 1))
    far = sum(1 for axis, _ in device_bits() if axis == "fsdp")
    one.step()
    (one.value, pick_t, fc_in, fc_out) = fence(one.value, pick_t, fc_in, fc_out)
    fc_up = fc_in.reshape(rows, n_all, FF_PARTS, rows).swapaxes(1, 2).reshape(rows, FF)
    fc_down = fc_out.reshape(FF_PARTS, rows, D).swapaxes(0, 1).reshape(rows, FF)
    w_fc = gather_rows(jnp.concatenate([fc_up, fc_down], axis=1))
    for _ in range(far - 2):
        one.step()
        (one.value, pick_t) = fence(one.value, pick_t)
    in_t = exchange(pick_t)
    pick_a = pick("pick_frames", (frames, 0))
    one.step()
    (one.value, in_t, pick_a) = fence(one.value, in_t, pick_a)
    in_a = exchange(pick_a)
    while len(one.left) > 1:
        one.send()
        pick_b = pick("pick_cotangent", (cotangent, 0))
        pick_c = pick("pick_third", (frames, 1), (cotangent, 1))
        (one.value, one.got, pick_b, pick_c) = fence(one.value, one.got, pick_b, pick_c)
        one.take()
    (w_one,) = one.step()
    (w_one, in_t) = fence(w_one, in_t)
    w_one = rows_of(w_one)
    norm_rows = w_one[:, ONE_NORM : ONE_NORM + 8].T.astype(f32)

    fwd0 = run_self_forward(len0, in_t, "first", w_one, norm_rows)
    fwd1 = run_self_forward(len1, in_t, "second", w_one, norm_rows)
    (in_a, fwd0, fwd1, pick_b) = fence(in_a, fwd0, fwd1, pick_b)
    in_b = exchange(pick_b)
    crs0 = run_cross_forward(len0, in_a, w_two, fwd0[6])
    (in_b, fwd0, crs0, pick_c) = fence(in_b, fwd0, crs0, pick_c)

    in_c = exchange(pick_c)
    mid0 = run_middle(len0, crs0[0], fwd0[4], in_b, "all", w_two, w_fc, norm_rows)
    cb0 = run_cross_backward(len0, fwd0[6], crs0[2], crs0[0], mid0[7], crs0[1], w_two, mid0[0])
    mid0 = mid0[1:]
    (in_c, crs0, cb0, fwd1, mid0) = fence(in_c, crs0, cb0, fwd1, mid0)

    lens = (len0, len1)

    back_a = exchange(cb0[2])
    crs1 = run_cross_forward(len1, in_c, w_two, fwd1[6])
    mid1 = run_middle(len1, crs1[0], fwd1[4], in_c, "tokens", w_two, w_fc, norm_rows)
    leaving, mid1 = mid1[0], mid1[1:]
    fc_sides = [(mid[0], mid[2], mid[1], mid[3]) for mid in (mid0, mid1)]
    g_fc = run_fc_grad(lens, *fc_sides)
    (crs1, mid1, g_fc, leaving) = fence(crs1, mid1, g_fc, leaving)
    g_fc = lax.psum_scatter(g_fc, ("grp", "fsdp"), scatter_dimension=0, tiled=True)
    cb1 = run_cross_backward(len1, fwd1[6], crs1[2], crs1[0], mid1[6], crs1[1], w_two, leaving)
    (back_a, cb0, cb1, mid0, mid1) = fence(back_a, cb0, cb1, mid0, mid1)

    back_b = exchange(cb1[2])
    sb0 = run_self_backward(
        len0, cb0[0], mid0[5], fwd0[4], fwd0[0], fwd0[2], fwd0[3], in_t, "first", w_one, norm_rows, None, 0
    )
    sb1 = run_self_backward(
        len1, cb1[0], mid1[5], fwd1[4], fwd1[0], fwd1[2], fwd1[3], in_t, "second", w_one, norm_rows, sb0[2], 1
    )
    halves = run_grad("grad_self_in", lens, ((fwd0[1], sb0[1]), (fwd1[1], sb1[1])), 5 * D, 0)
    halves = run_grad("grad_self_out", lens, ((fwd0[2], sb0[0]), (fwd1[2], sb1[0])), 5 * D, 3, halves)
    halves = run_grad("grad_cross_q", lens, ((fwd0[5], cb0[0]), (fwd1[5], cb1[0])), 5 * D, 4, halves)
    g_one = Scatter("one", *halves)
    gtok, sb0, sb1 = sb1[2], (sb0[0], sb0[1], sb0[3]), (sb1[0], sb1[1], sb1[3])
    (sb0, sb1, g_one.keep, g_one.send, cb0, cb1, mid0, mid1) = fence(
        sb0, sb1, g_one.keep, g_one.send, cb0, cb1, mid0, mid1
    )
    g_one.step()
    halves = run_grad("grad_cross_kv", lens, ((in_a, cb0[1]), (in_c, cb1[1])), 3 * D + PAIR, 0, full=True)
    (g_one.keep, g_one.send, halves, cb0, cb1) = fence(g_one.keep, g_one.send, halves, cb0, cb1)
    g_one.move()
    halves = run_grad(
        "grad_cross_out", lens, ((crs0[0], mid0[4]), (crs1[0], mid1[4])), 3 * D + PAIR, 2, halves
    )
    ng_self = sb0[2] + sb1[2]
    ng_mid = mid0[7] + mid1[7]
    norm_sum = jnp.concatenate([ng_self[:2], ng_mid[:2], ng_self[2:4], ng_mid[2:4]], axis=0)
    g_two = Scatter("two", *put_norm_grad(norm_sum, halves))
    g_two.move()
    (back_b, g_two.got, gtok) = fence(back_b, g_two.got, gtok)

    back_c = exchange(gtok)
    grad_frames, output = put_back(
        "put_frames",
        (back_a, slice(0, 3 * size), back_b, slice(0, 3 * size)),
        (back_a, slice(3 * size, 4 * size), back_b, slice(3 * size, 4 * size)),
    )
    g_one = g_one.finish()
    g_two = g_two.finish()
    g_norm = g_two[:, 3 * D : 3 * D + 8]
    (grad_tokens,) = put_back("put_tokens", (back_c, slice(0, size), back_c, slice(size, 2 * size)))
    return (
        output,
        grad_tokens,
        grad_frames,
        by_part(g_one[:, :ONE_OUT], 3),
        g_one[:, ONE_OUT:ONE_Q],
        g_one[:, ONE_Q:],
        by_part(g_two[:, :TWO_OUT], 2),
        g_two[:, TWO_OUT : 3 * D],
        g_fc[:, :FF].astype(f32).reshape(rows, FF_PARTS, n_all, rows).swapaxes(1, 2).reshape(rows, FF),
        g_fc[:, FF:].astype(f32).reshape(rows, FF_PARTS, D).swapaxes(0, 1).reshape(FF_PARTS * rows, D),
        g_norm[:, :4],
        g_norm[:, 4:],
    )


def solution(mesh):
    rows = P(("grp", "fsdp"), None)
    seqs = P("grp", "fsdp", None)
    return jax.shard_map(
        shards,
        mesh=mesh,
        in_specs=(seqs, seqs, P("grp"), seqs) + (rows,) * 9,
        out_specs=(seqs,) * 3 + (rows,) * 9,
        check_vma=False,
    )
```

profile of v0, /device:TPU:0, one launch (start us, length us, event | category | flops | bytes accessed | tf_op | source)
XLA Modules:
  0.0 632.1 jit_solution(5112153895254336273)
XLA Ops:
  13.0 4.1 collective-permute-start
  20.7 3.7 pick_tokens.1
  31.5 10.0 %collective-permute-done.1.refs_1_ = bf16[2,24,3968]{2,1,0:T(8,128)(2,1)S(1)} collective-permute-done((bf16[2,24,3968]{2,1,0:T(8,128)(2,1)S(1)}, bf16[2,24,3968]{2,1,0:T(8,128)(2,1)S(1)}, u32[]{:S(2)}, u32[]{:S(2)}) %collective-permute-start.1) | collective-permute-done | bytes 380960 | tf_op jit(solution)/shard_map/ppermute | solution.py:620
  42.4 6.1 all-to-all-start
  55.3 34.4 %collective-permute-done.2.refs_1_ = bf16[4,24,3968]{2,1,0:T(8,128)(2,1)S(1)} collective-permute-done((bf16[4,24,3968]{2,1,0:T(8,128)(2,1)S(1)}, bf16[4,24,3968]{2,1,0:T(8,128)(2,1)S(1)}, u32[]{:S(2)}, u32[]{:S(2)}) %collective-permute-start.2) | collective-permute-done | bytes 761888 | tf_op jit(solution)/shard_map/ppermute | solution.py:620
  90.9 5.0 all-to-all-done.tok_ref.refs_7_
  97.2 4.4 all-to-all-start.1
  103.9 3.7 pick_third.1
  107.7 2.5 pick_cotangent.1
  110.2 22.5 %collective-permute-done.3.refs_1_ = bf16[8,24,3968]{2,1,0:T(8,128)(2,1)} collective-permute-done((bf16[8,24,3968]{2,1,0:T(8,128)(2,1)}, bf16[8,24,3968]{2,1,0:T(8,128)(2,1)}, u32[]{:S(2)}, u32[]{:S(2)}) %collective-permute-start.3) | collective-permute-done | bytes 1523744 | tf_op jit(solution)/shard_map/ppermute | solution.py:620
  132.6 3.0 one_join.7.refs_0_
  137.1 4.5 collective-permute-done.4.refs_1_
  143.7 4.4 one_order.1
  149.3 2.7 copy-done
  152.0 7.9 %self_part_forward.3 = (bf16[512,2304]{1,0:T(8,128)(2,1)}, bf16[512,768]{1,0:T(8,128)(2,1)}, bf16[512,768]{1,0:T(8,128)(2,1)}, f32[6,4,256]{2,1,0:T(4,128)}, f32...) custom-call(s32[1]{0:T(128)} %get-tuple-element.428.len_ref.len1_ref, ...), custom_call_target="tpu_custom_call" | custom-call | flops 1000000 | bytes 1000000 | tf_op jit(solution)/shard_map/self_part_forward/pallas_call | solution.py:215
  159.9 18.4 %self_part_forward.2 = (bf16[512,2304]{1,0:T(8,128)(2,1)}, bf16[512,768]{1,0:T(8,128)(2,1)}, bf16[512,768]{1,0:T(8,128)(2,1)}, f32[6,4,256]{2,1,0:T(4,128)}, f32...) custom-call(s32[1]{0:T(128)} %get-tuple-element.429.len_ref.len0_ref.refs_0_, ...), custom_call_target="tpu_custom_call" | custom-call | flops 1000000 | bytes 1000000 | tf_op jit(solution)/shard_map/self_part_forward/pallas_call | solution.py:215
  178.3 3.5 all-to-all-start.2
  185.0 23.8 %cross_forward.2 = (bf16[512,768]{1,0:T(8,128)(2,1)}, f32[6,2,512]{2,1,0:T(2,128)}, bf16[1536,1536]{1,0:T(8,128)(2,1)}) custom-call(s32[1]{0:T(128)} %get-tuple-element.429.len_ref.len0_ref.refs_0_, bf16[8,192,768]{2,1,0:T(8,128)(2,1)} %all-to-all-done.1.frm_ref.left0_ref, bf16[768,2304]{1,0:T(8,128)(2,1)S(1)} %copy-done.1, bf16[512,768]{1,0:T(8,128)(2,1)S(1)} %copy-done.39), custom_call_target="tpu_custom_call" | custom-call | flops 1000000 | bytes 1000000 | tf_op jit(solution)/shard_map/cross_forward/pallas_call | solution.py:271
  208.9 7.5 %all-to-all-done.2.cot_ref = bf16[8,64,768]{2,1,0:T(8,128)(2,1)S(1)} async-done(((bf16[8,64,768]{2,1,0:T(8,128)(2,1)}), bf16[8,64,768]{2,1,0:T(8,128)(2,1)S(1)}, u32[]{:S(2)}, u32[]{:S(2)}) %all-to-all-start.2) | async-done | bytes 786464 | tf_op jit(solution)/shard_map/all_to_all | solution.py:972
  217.3 4.9 all-to-all-start.3
  226.6 24.6 %mlp_and_back.2 = (bf16[8,256,768]{2,1,0:T(8,128)(2,1)}, bf16[512,768]{1,0:T(8,128)(2,1)}, bf16[512,3072]{1,0:T(8,128)(2,1)}, bf16[512,3072]{1,0:T(8,128)(2,1)},...) custom-call(s32[1]{0:T(128)} %get-tuple-element.429.len_ref.len0_ref, ...), custom_call_target="tpu_custom_call" | custom-call | flops 1000000 | bytes 1000000 | tf_op jit(solution)/shard_map/mlp_and_back/pallas_call | solution.py:452
  252.4 36.8 %cross_backward.2 = (bf16[512,768]{1,0:T(8,128)(2,1)}, bf16[1536,1536]{1,0:T(8,128)(2,1)}, bf16[8,256,768]{2,1,0:T(8,128)(2,1)}) custom-call(s32[1]{0:T(128)} %get-tuple-element.429.len_ref.len0_ref.refs_0_, bf16[512,768]{1,0:T(8,128)(2,1)S(1)} %copy-done.40, bf16[1536,1536]{1,0:T(8,128)(2,1)S(1)} %copy-done.24, ...), custom_call_target="tpu_custom_call", output_to_operand_aliasing={{2}: (7, {})} | custom-call | flops 1000000 | bytes 1000000 | tf_op jit(solution)/shard_map/cross_backward/pallas_call | solution.py:348
  289.2 3.7 all-to-all-done.3.frm_ref.cot_ref.left1_ref
  292.9 4.4 all-to-all-start.4
  298.5 15.9 %cross_forward.3 = (bf16[512,768]{1,0:T(8,128)(2,1)}, f32[6,2,512]{2,1,0:T(2,128)}, bf16[1536,1536]{1,0:T(8,128)(2,1)}) custom-call(s32[1]{0:T(128)} %get-tuple-element.428.len_ref.len1_ref, bf16[8,256,768]{2,1,0:T(8,128)(2,1)} %all-to-all-done.3.frm_ref.cot_ref.left1_ref, bf16[768,2304]{1,0:T(8,128)(2,1)S(1)} %copy-done.2, bf16[512,768]{1,0:T(8,128)(2,1)S(1)} %copy-done.37), custom_call_target="tpu_custom_call" | custom-call | flops 1000000 | bytes 1000000 | tf_op jit(solution)/shard_map/cross_forward/pallas_call | solution.py:271
  315.6 16.8 %mlp_and_back.3 = (bf16[8,256,768]{2,1,0:T(8,128)(2,1)}, bf16[512,768]{1,0:T(8,128)(2,1)}, bf16[512,3072]{1,0:T(8,128)(2,1)}, bf16[512,3072]{1,0:T(8,128)(2,1)},...) custom-call(s32[1]{0:T(128)} %get-tuple-element.428.len_ref.len1_ref, ...), custom_call_target="tpu_custom_call" | custom-call | flops 1000000 | bytes 1000000 | tf_op jit(solution)/shard_map/mlp_and_back/pallas_call | solution.py:452
  338.6 17.4 %grad_fc.1 = bf16[768,6144]{1,0:T(8,128)(2,1)} custom-call(s32[1]{0:T(128)} %get-tuple-element.429.len_ref.len0_ref.refs_0_, s32[1]{0:T(128)} %get-tuple-element.428.len_ref.len1_ref, bf16[512,768]{1,0:T(8,128)(2,1)S(1)} %copy-done.58, bf16[512,3072]{1,0:T(8,128)(2,1)S(1)} %copy-done.34, bf16[512,3072]{1,0:T(8,128)(2,1)S(1)} %copy-done.33, ...), custom_call_target="tpu_custom_call" | custom-call | flops 1000000 | bytes 1000000 | tf_op jit(solution)/shard_map/grad_fc/pallas_call | solution.py:836
  364.4 22.2 %cross_backward.3 = (bf16[512,768]{1,0:T(8,128)(2,1)}, bf16[1536,1536]{1,0:T(8,128)(2,1)}, bf16[8,256,768]{2,1,0:T(8,128)(2,1)}) custom-call(s32[1]{0:T(128)} %get-tuple-element.428.len_ref.len1_ref, bf16[512,768]{1,0:T(8,128)(2,1)S(1)} %copy-done.38, bf16[1536,1536]{1,0:T(8,128)(2,1)S(1)} %copy-done.23, ...), custom_call_target="tpu_custom_call", output_to_operand_aliasing={{2}: (7, {})} | custom-call | flops 1000000 | bytes 1000000 | tf_op jit(solution)/shard_map/cross_backward/pallas_call | solution.py:348
  386.6 10.5 %all-to-all-start.5 = ((bf16[8,256,768]{2,1,0:T(8,128)(2,1)}), bf16[8,256,768]{2,1,0:T(8,128)(2,1)}, u32[]{:S(2)}, u32[]{:S(2)}) async-start(bf16[8,256,768]{2,1,0:T(8,128)(2,1)} %get-tuple-element.304), calls=%async_computation.5 | async-start | bytes 6291456 | tf_op jit(solution)/shard_map/all_to_all | solution.py:972
  402.9 21.4 %self_part_backward.2 = (bf16[512,768]{1,0:T(8,128)(2,1)}, bf16[512,2304]{1,0:T(8,128)(2,1)}, bf16[8,128,768]{2,1,0:T(8,128)(2,1)}, f32[8,768]{1,0:T(8,128)}) custom-call(s32[1]{0:T(128)} %get-tuple-element.429.len_ref.len0_ref.refs_0_, bf16[512,768]{1,0:T(8,128)(2,1)S(1)} %copy-done.28, f32[512,768]{1,0:T(8,128)S(1)} %copy-done.47, ...), custom_call_target="tpu_custom_call" | custom-call | flops 1000000 | bytes 1000000 | tf_op jit(solution)/shard_map/self_part_backward/pallas_call | solution.py:557
  424.4 10.9 %self_part_backward.3 = (bf16[512,768]{1,0:T(8,128)(2,1)}, bf16[512,2304]{1,0:T(8,128)(2,1)}, bf16[8,128,768]{2,1,0:T(8,128)(2,1)}, f32[8,768]{1,0:T(8,128)}) custom-call(s32[1]{0:T(128)} %get-tuple-element.428.len_ref.len1_ref, bf16[512,768]{1,0:T(8,128)(2,1)S(1)} %copy-done.30, f32[512,768]{1,0:T(8,128)S(1)} %copy-done.48, ...), custom_call_target="tpu_custom_call", output_to_operand_aliasing={{2}: (10, {})} | custom-call | flops 1000000 | bytes 1000000 | tf_op jit(solution)/shard_map/self_part_backward/pallas_call | solution.py:557
  435.3 8.7 %grad_self_in.1 = (bf16[2,192,3840]{2,1,0:T(8,128)(2,1)}, bf16[2,192,3840]{2,1,0:T(8,128)(2,1)}) custom-call(s32[1]{0:T(128)} %get-tuple-element.429.len_ref.len0_ref.refs_0_, s32[1]{0:T(128)} %get-tuple-element.428.len_ref.len1_ref, s32[1]{0:T(128)} %bitcast.10.bit_ref, bf16[512,768]{1,0:T(8,128)(2,1)S(1)} %copy-done.71, bf16[512,2304]{1,0:T(8,128)(2,1)S(1)} %copy-done.43, ...), custom_call_target="tpu_custom_call" | custom-call | flops 1000000 | bytes 1000000 | tf_op jit(solution)/shard_map/grad_self_in/pallas_call | solution.py:864
  444.1 4.4 grad_self_out.1
  448.6 4.2 grad_cross_q.1
  452.9 15.7 %grad_cross_kv.1 = (bf16[2,192,2432]{2,1,0:T(8,128)(2,1)}, bf16[2,192,2432]{2,1,0:T(8,128)(2,1)}) custom-call(s32[1]{0:T(128)} %get-tuple-element.429.len_ref.len0_ref.refs_0_, s32[1]{0:T(128)} %get-tuple-element.428.len_ref.len1_ref, s32[1]{0:T(128)} %bitcast.10.bit_ref, bf16[8,192,768]{2,1,0:T(8,128)(2,1)} %all-to-all-done.1.frm_ref.left0_ref, ...), custom_call_target="tpu_custom_call" | custom-call | flops 1000000 | bytes 1000000 | tf_op jit(solution)/shard_map/grad_cross_kv/pallas_call | solution.py:864
  471.8 4.4 grad_cross_out.1
  477.6 30.1 %collective-permute-start.7 = (bf16[8,24,3840]{2,1,0:T(8,128)(2,1)}, bf16[8,24,3840]{2,1,0:T(8,128)(2,1)}, u32[]{:S(2)}, u32[]{:S(2)}) collective-permute-start(bf16[8,24,3840]{2,1,0:T(8,128)(2,1)} %bitcast.17), channel_id=1, source_target_pairs={{0,16},{8,24},{16,0},{24,8},{1,17},{9,25},{17,1},{25,9},{2,18},{10... | collective-permute-start | bytes 4423688 | tf_op jit(solution)/shard_map/ppermute | solution.py:620
  509.0 13.3 %all-to-all-start.6 = ((bf16[8,128,768]{2,1,0:T(8,128)(2,1)}), bf16[8,128,768]{2,1,0:T(8,128)(2,1)S(1)}, u32[]{:S(2)}, u32[]{:S(2)}) async-start(bf16[8,128,768]{2,1,0:T(8,128)(2,1)} %get-tuple-element.361), calls=%async_computation.6 | async-start | bytes 3145728 | tf_op jit(solution)/shard_map/all_to_all | solution.py:972
  526.2 3.7 collective-permute-start.11
  529.9 19.7 %collective-permute-done.7 = bf16[8,24,3840]{2,1,0:T(8,128)(2,1)} collective-permute-done((bf16[8,24,3840]{2,1,0:T(8,128)(2,1)}, bf16[8,24,3840]{2,1,0:T(8,128)(2,1)}, u32[]{:S(2)}, u32[]{:S(2)}) %collective-permute-start.7) | collective-permute-done | bytes 1474592 | tf_op jit(solution)/shard_map/ppermute | solution.py:620
  551.0 3.5 one_add.5
  556.8 20.1 %collective-permute-done.8 = bf16[4,24,3840]{2,1,0:T(8,128)(2,1)} collective-permute-done((bf16[4,24,3840]{2,1,0:T(8,128)(2,1)}, bf16[4,24,3840]{2,1,0:T(8,128)(2,1)}, u32[]{:S(2)}, u32[]{:S(2)}) %collective-permute-start.8) | collective-permute-done | bytes 737312 | tf_op jit(solution)/shard_map/ppermute | solution.py:620
  579.8 2.5 collective-permute-start.9
  584.6 6.9 %collective-permute-done.9 = bf16[2,24,3840]{2,1,0:T(8,128)(2,1)} collective-permute-done((bf16[2,24,3840]{2,1,0:T(8,128)(2,1)}, bf16[2,24,3840]{2,1,0:T(8,128)(2,1)}, u32[]{:S(2)}, u32[]{:S(2)}) %collective-permute-start.9) | collective-permute-done | bytes 368672 | tf_op jit(solution)/shard_map/ppermute | solution.py:620
  593.6 2.8 collective-permute-start.10
  598.8 5.5 put_frames.1
  612.0 3.8 copy.68
  615.9 4.0 reshape.307
  (279 shorter events, 101.8 us)
Async XLA Ops:
  7.2 174.7 %all-gather.3.cloned.1.call-start = ((), (), s32[]{:S(2)}) async-start(), calls=%async_computation.8 | async-start | bytes 3649536 | tf_op jit(solution)/shard_map/all_gather | solution.py:706
  13.0 209.2 %all-gather.5.cloned.1.call-start = ((), (), s32[]{:S(2)}) async-start(), calls=%async_computation.9 | async-start | bytes 9732096 | tf_op jit(solution)/shard_map/all_gather | solution.py:706
  13.0 13.2 %collective-permute-start = (bf16[1,24,3968]{2,1,0:T(8,128)(2,1)}, bf16[1,24,3968]{2,1,0:T(8,128)(2,1)S(1)}, u32[]{:S(2)}, u32[]{:S(2)}) collective-permute-start(bf16[1,24,3968]{2,1,0:T(8,128)(2,1)} %bitcast.84), channel_id=1, source_target_pairs={{0,4},{1,5},{2,6},{3,7},{4,0},{5,1},{6,2},{7,3},{8,12},{9,13},{10,... | collective-permute-start | bytes 571400 | tf_op jit(solution)/shard_map/ppermute | solution.py:620
  30.5 11.1 %collective-permute-start.1 = (bf16[2,24,3968]{2,1,0:T(8,128)(2,1)S(1)}, bf16[2,24,3968]{2,1,0:T(8,128)(2,1)S(1)}, u32[]{:S(2)}, u32[]{:S(2)}) collective-permute-start(bf16[2,24,3968]{2,1,0:T(8,128)(2,1)S(1)} %copy-done.49), channel_id=1, source_target_pairs={{0,2},{1,3},{2,0},{3,1},{4,6},{5,7},{6,4},{7,5},{8,10},{9,11},{10,... | collective-permute-start | bytes 1142792 | tf_op jit(solution)/shard_map/ppermute | solution.py:620
  42.4 53.4 %all-to-all-start = ((bf16[8,128,768]{2,1,0:T(8,128)(2,1)}), bf16[8,128,768]{2,1,0:T(8,128)(2,1)S(1)}, u32[]{:S(2)}, u32[]{:S(2)}) async-start(bf16[8,128,768]{2,1,0:T(8,128)(2,1)} %pick_tokens.1), calls=%async_computation | async-start | bytes 3145728 | tf_op jit(solution)/shard_map/all_to_all | solution.py:972
  48.5 41.2 %collective-permute-start.2 = (bf16[4,24,3968]{2,1,0:T(8,128)(2,1)S(1)}, bf16[4,24,3968]{2,1,0:T(8,128)(2,1)S(1)}, u32[]{:S(2)}, u32[]{:S(2)}) collective-permute-start(bf16[4,24,3968]{2,1,0:T(8,128)(2,1)S(1)} %copy-done.41), channel_id=1, source_target_pairs={{0,1},{1,0},{2,3},{3,2},{4,5},{5,4},{6,7},{7,6},{8,9},{9,8},{10,11... | collective-permute-start | bytes 2285576 | tf_op jit(solution)/shard_map/ppermute | solution.py:620
  95.9 64.0 %copy-start.4 = (bf16[8,128,768]{2,1,0:T(8,128)(2,1)}, bf16[8,128,768]{2,1,0:T(8,128)(2,1)S(1)}, u32[]{:S(2)}) copy-start(bf16[8,128,768]{2,1,0:T(8,128)(2,1)S(1)} %all-to-all-done.tok_ref.refs_7_) | copy-start | bytes 4718596
  95.9 36.8 %collective-permute-start.3 = (bf16[8,24,3968]{2,1,0:T(8,128)(2,1)}, bf16[8,24,3968]{2,1,0:T(8,128)(2,1)}, u32[]{:S(2)}, u32[]{:S(2)}) collective-permute-start(bf16[8,24,3968]{2,1,0:T(8,128)(2,1)} %one_join.6.refs_0_), channel_id=1, source_target_pairs={{0,16},{8,24},{16,0},{24,8},{1,17},{9,25},{17,1},{25,9},{2,18},{10... | collective-permute-start | bytes 4571144 | tf_op jit(solution)/shard_map/ppermute | solution.py:620
  97.2 81.1 %all-to-all-start.1 = ((bf16[8,192,768]{2,1,0:T(8,128)(2,1)}), bf16[8,192,768]{2,1,0:T(8,128)(2,1)}, u32[]{:S(2)}, u32[]{:S(2)}) async-start(bf16[8,192,768]{2,1,0:T(8,128)(2,1)} %pick_frames.1), calls=%async_computation.1 | async-start | bytes 4718592 | tf_op jit(solution)/shard_map/all_to_all | solution.py:972
  107.7 25.0 %copy-start.22 = (bf16[8,24,3968]{2,1,0:T(8,128)(2,1)S(1)}, bf16[8,24,3968]{2,1,0:T(8,128)(2,1)}, u32[]{:S(2)}) copy-start(bf16[8,24,3968]{2,1,0:T(8,128)(2,1)} %one_join.6.refs_0_) | copy-start | bytes 4571140
  110.2 25.7 %copy-start.88 = (s32[16]{0:T(128)S(1)}, s32[16]{0:T(128)}, u32[]{:S(2)}) copy-start(s32[16]{0:T(128)} %param.15) | copy-start | bytes 196
  135.7 5.9 collective-permute-start.4
  178.3 38.1 %all-to-all-start.2 = ((bf16[8,64,768]{2,1,0:T(8,128)(2,1)}), bf16[8,64,768]{2,1,0:T(8,128)(2,1)S(1)}, u32[]{:S(2)}, u32[]{:S(2)}) async-start(bf16[8,64,768]{2,1,0:T(8,128)(2,1)} %pick_cotangent.1), calls=%async_computation.2 | async-start | bytes 1572864 | tf_op jit(solution)/shard_map/all_to_all | solution.py:972
  217.3 75.6 %all-to-all-start.3 = ((bf16[8,256,768]{2,1,0:T(8,128)(2,1)}), bf16[8,256,768]{2,1,0:T(8,128)(2,1)}, u32[]{:S(2)}, u32[]{:S(2)}) async-start(bf16[8,256,768]{2,1,0:T(8,128)(2,1)} %pick_third.1), calls=%async_computation.3 | async-start | bytes 6291456 | tf_op jit(solution)/shard_map/all_to_all | solution.py:972
  226.6 24.6 %copy-start.2 = (bf16[768,2304]{1,0:T(8,128)(2,1)S(1)}, bf16[768,2304]{1,0:T(8,128)(2,1)}, u32[]{:S(2)}) copy-start(bf16[768,2304]{1,0:T(8,128)(2,1)} %all-gather.3.cloned.1.call-done.w_ref.two_ref) | copy-start | bytes 10616836
  226.6 24.6 %copy-start.24 = (bf16[1536,1536]{1,0:T(8,128)(2,1)S(1)}, bf16[1536,1536]{1,0:T(8,128)(2,1)}, u32[]{:S(2)}) copy-start(bf16[1536,1536]{1,0:T(8,128)(2,1)} %get-tuple-element.242.kv_ref) | copy-start | bytes 14155780
  226.6 24.6 %copy-start.40 = (bf16[512,768]{1,0:T(8,128)(2,1)S(1)}, bf16[512,768]{1,0:T(8,128)(2,1)}, u32[]{:S(2)}) copy-start(bf16[512,768]{1,0:T(8,128)(2,1)} %get-tuple-element.243.q_ref) | copy-start | bytes 2359300
  226.6 24.6 %copy-start.86 = (f32[6,2,512]{2,1,0:T(2,128)S(1)}, f32[6,2,512]{2,1,0:T(2,128)}, u32[]{:S(2)}) copy-start(f32[6,2,512]{2,1,0:T(2,128)} %get-tuple-element.241.lse_ref) | copy-start | bytes 73732
  292.9 93.7 %all-to-all-start.4 = ((bf16[8,256,768]{2,1,0:T(8,128)(2,1)}), bf16[8,256,768]{2,1,0:T(8,128)(2,1)}, u32[]{:S(2)}, u32[]{:S(2)}) async-start(bf16[8,256,768]{2,1,0:T(8,128)(2,1)} %get-tuple-element.267), calls=%async_computation.4 | async-start | bytes 6291456 | tf_op jit(solution)/shard_map/all_to_all | solution.py:972
  297.4 311.4 %reduce-scatter.2.cloned.1.call-start = ((), (), s32[]{:S(2)}) async-start(), calls=%async_computation.10 | async-start | bytes 9732096 | tf_op jit(solution)/shard_map/reduce_scatter | solution.py:1092
  298.5 15.9 %copy-start.20 = (f32[512,768]{1,0:T(8,128)S(1)}, f32[512,768]{1,0:T(8,128)}, u32[]{:S(2)}) copy-start(f32[512,768]{1,0:T(8,128)} %get-tuple-element.275.after_ref) | copy-start | bytes 4718596
  298.5 15.9 %copy-start.54 = (f32[8,768]{1,0:T(8,128)S(1)}, f32[8,768]{1,0:T(8,128)}, u32[]{:S(2)}) copy-start(f32[8,768]{1,0:T(8,128)} %copy-done.52) | copy-start | bytes 73732
  315.6 16.9 %copy-start.33 = (bf16[512,3072]{1,0:T(8,128)(2,1)S(1)}, bf16[512,3072]{1,0:T(8,128)(2,1)}, u32[]{:S(2)}) copy-start(bf16[512,3072]{1,0:T(8,128)(2,1)} %get-tuple-element.286.hid0_ref) | copy-start | bytes 9437188
  315.6 16.9 %copy-start.34 = (bf16[512,3072]{1,0:T(8,128)(2,1)S(1)}, bf16[512,3072]{1,0:T(8,128)(2,1)}, u32[]{:S(2)}) copy-start(bf16[512,3072]{1,0:T(8,128)(2,1)} %get-tuple-element.285.pre0_ref) | copy-start | bytes 9437188
  315.6 16.9 %copy-start.58 = (bf16[512,768]{1,0:T(8,128)(2,1)S(1)}, bf16[512,768]{1,0:T(8,128)(2,1)}, u32[]{:S(2)}) copy-start(bf16[512,768]{1,0:T(8,128)(2,1)} %get-tuple-element.284.normed0_ref) | copy-start | bytes 2359300
  315.6 16.9 %copy-start.59 = (bf16[512,768]{1,0:T(8,128)(2,1)S(1)}, bf16[512,768]{1,0:T(8,128)(2,1)}, u32[]{:S(2)}) copy-start(bf16[512,768]{1,0:T(8,128)(2,1)} %get-tuple-element.287.branch0_ref) | copy-start | bytes 2359300
  386.6 122.3 %all-to-all-start.5 = ((bf16[8,256,768]{2,1,0:T(8,128)(2,1)}), bf16[8,256,768]{2,1,0:T(8,128)(2,1)}, u32[]{:S(2)}, u32[]{:S(2)}) async-start(bf16[8,256,768]{2,1,0:T(8,128)(2,1)} %get-tuple-element.304), calls=%async_computation.5 | async-start | bytes 6291456 | tf_op jit(solution)/shard_map/all_to_all | solution.py:972
  402.9 21.4 %copy-start.21 = (f32[512,768]{1,0:T(8,128)S(1)}, f32[512,768]{1,0:T(8,128)}, u32[]{:S(2)}) copy-start(f32[512,768]{1,0:T(8,128)} %get-tuple-element.275.after_ref) | copy-start | bytes 4718596
  402.9 21.4 %copy-start.25 = (bf16[512,768]{1,0:T(8,128)(2,1)S(1)}, bf16[512,768]{1,0:T(8,128)(2,1)}, u32[]{:S(2)}) copy-start(bf16[512,768]{1,0:T(8,128)(2,1)} %get-tuple-element.316.mix_ref.left1_ref) | copy-start | bytes 2359300
  402.9 21.4 %copy-start.30 = (bf16[512,768]{1,0:T(8,128)(2,1)S(1)}, bf16[512,768]{1,0:T(8,128)(2,1)}, u32[]{:S(2)}) copy-start(bf16[512,768]{1,0:T(8,128)(2,1)} %get-tuple-element.313.dq_ref.right1_ref) | copy-start | bytes 2359300
  402.9 21.4 %copy-start.44 = (bf16[512,2304]{1,0:T(8,128)(2,1)S(1)}, bf16[512,2304]{1,0:T(8,128)(2,1)}, u32[]{:S(2)}) copy-start(bf16[512,2304]{1,0:T(8,128)(2,1)} %get-tuple-element.315.qkv_ref) | copy-start | bytes 7077892
  402.9 21.4 %copy-start.48 = (f32[512,768]{1,0:T(8,128)S(1)}, f32[512,768]{1,0:T(8,128)}, u32[]{:S(2)}) copy-start(f32[512,768]{1,0:T(8,128)} %get-tuple-element.314.grad_cross_ref) | copy-start | bytes 4718596
  402.9 21.4 %copy-start.87 = (f32[6,4,256]{2,1,0:T(4,128)S(1)}, f32[6,4,256]{2,1,0:T(4,128)}, u32[]{:S(2)}) copy-start(f32[6,4,256]{2,1,0:T(4,128)} %get-tuple-element.317.lse_ref) | copy-start | bytes 73732
  424.3 11.0 %copy-start.43 = (bf16[512,2304]{1,0:T(8,128)(2,1)S(1)}, bf16[512,2304]{1,0:T(8,128)(2,1)}, u32[]{:S(2)}) copy-start(bf16[512,2304]{1,0:T(8,128)(2,1)} %get-tuple-element.311.right0_ref) | copy-start | bytes 7077892
  452.8 15.8 %collective-permute-start.5 = (bf16[16,24,3840]{2,1,0:T(8,128)(2,1)}, bf16[16,24,3840]{2,1,0:T(8,128)(2,1)S(1)}, u32[]{:S(2)}, u32[]{:S(2)}) collective-permute-start(bf16[16,24,3840]{2,1,0:T(8,128)(2,1)} %bitcast.91), channel_id=1, source_target_pairs={{0,8},{8,0},{16,24},{24,16},{1,9},{9,1},{17,25},{25,17},{2,10},{10... | collective-permute-start | bytes 8847368 | tf_op jit(solution)/shard_map/ppermute | solution.py:620
  452.9 15.8 %copy-start.6 = (bf16[2,192,3840]{2,1,0:T(8,128)(2,1)S(1)}, bf16[2,192,3840]{2,1,0:T(8,128)(2,1)}, u32[]{:S(2)}) copy-start(bf16[2,192,3840]{2,1,0:T(8,128)(2,1)} %get-tuple-element.330) | copy-start | bytes 8847364
  477.1 45.1 %copy-start.9 = (bf16[2,192,2432]{2,1,0:T(8,128)(2,1)S(1)}, bf16[2,192,2432]{2,1,0:T(8,128)(2,1)}, u32[]{:S(2)}) copy-start(bf16[2,192,2432]{2,1,0:T(8,128)(2,1)} %get-tuple-element.371) | copy-start | bytes 5603332
  477.1 30.6 %collective-permute-start.6 = (bf16[16,24,2432]{2,1,0:T(8,128)(2,1)}, bf16[16,24,2432]{2,1,0:T(8,128)(2,1)S(1)}, u32[]{:S(2)}, u32[]{:S(2)}) collective-permute-start(bf16[16,24,2432]{2,1,0:T(8,128)(2,1)} %bitcast.92), channel_id=1, source_target_pairs={{0,8},{8,0},{16,24},{24,16},{1,9},{9,1},{17,25},{25,17},{2,10},{10... | collective-permute-start | bytes 5603336 | tf_op jit(solution)/shard_map/ppermute | solution.py:620
  477.6 72.0 %collective-permute-start.7 = (bf16[8,24,3840]{2,1,0:T(8,128)(2,1)}, bf16[8,24,3840]{2,1,0:T(8,128)(2,1)}, u32[]{:S(2)}, u32[]{:S(2)}) collective-permute-start(bf16[8,24,3840]{2,1,0:T(8,128)(2,1)} %bitcast.17), channel_id=1, source_target_pairs={{0,16},{8,24},{16,0},{24,8},{1,17},{9,25},{17,1},{25,9},{2,18},{10... | collective-permute-start | bytes 4423688 | tf_op jit(solution)/shard_map/ppermute | solution.py:620
  509.0 114.7 %all-to-all-start.6 = ((bf16[8,128,768]{2,1,0:T(8,128)(2,1)}), bf16[8,128,768]{2,1,0:T(8,128)(2,1)S(1)}, u32[]{:S(2)}, u32[]{:S(2)}) async-start(bf16[8,128,768]{2,1,0:T(8,128)(2,1)} %get-tuple-element.361), calls=%async_computation.6 | async-start | bytes 3145728 | tf_op jit(solution)/shard_map/all_to_all | solution.py:972
  526.2 56.1 %collective-permute-start.11 = (bf16[8,24,2432]{2,1,0:T(8,128)(2,1)}, bf16[8,24,2432]{2,1,0:T(8,128)(2,1)S(1)}, u32[]{:S(2)}, u32[]{:S(2)}) collective-permute-start(bf16[8,24,2432]{2,1,0:T(8,128)(2,1)} %bitcast.37), channel_id=1, source_target_pairs={{0,16},{8,24},{16,0},{24,8},{1,17},{9,25},{17,1},{25,9},{2,18},{10... | collective-permute-start | bytes 2801672 | tf_op jit(solution)/shard_map/ppermute | solution.py:620
  551.0 31.4 %copy-start.57 = (bf16[1,8,24,2432]{3,2,1,0:T(8,128)(2,1)S(1)}, bf16[1,8,24,2432]{3,2,1,0:T(8,128)(2,1)}, u32[]{:S(2)}) copy-start(bf16[1,8,24,2432]{3,2,1,0:T(8,128)(2,1)} %copy-done.56) | copy-start | bytes 2801668
  555.4 21.5 %collective-permute-start.8 = (bf16[4,24,3840]{2,1,0:T(8,128)(2,1)}, bf16[4,24,3840]{2,1,0:T(8,128)(2,1)}, u32[]{:S(2)}, u32[]{:S(2)}) collective-permute-start(bf16[4,24,3840]{2,1,0:T(8,128)(2,1)} %bitcast.25), channel_id=1, source_target_pairs={{0,1},{1,0},{2,3},{3,2},{4,5},{5,4},{6,7},{7,6},{8,9},{9,8},{10,11... | collective-permute-start | bytes 2211848 | tf_op jit(solution)/shard_map/ppermute | solution.py:620
  579.8 11.7 %collective-permute-start.9 = (bf16[2,24,3840]{2,1,0:T(8,128)(2,1)}, bf16[2,24,3840]{2,1,0:T(8,128)(2,1)}, u32[]{:S(2)}, u32[]{:S(2)}) collective-permute-start(bf16[2,24,3840]{2,1,0:T(8,128)(2,1)} %bitcast.28), channel_id=1, source_target_pairs={{0,2},{1,3},{2,0},{3,1},{4,6},{5,7},{6,4},{7,5},{8,10},{9,11},{10,... | collective-permute-start | bytes 1105928 | tf_op jit(solution)/shard_map/ppermute | solution.py:620
  584.5 12.6 %collective-permute-start.12 = (bf16[4,24,2432]{2,1,0:T(8,128)(2,1)}, bf16[4,24,2432]{2,1,0:T(8,128)(2,1)S(1)}, u32[]{:S(2)}, u32[]{:S(2)}) collective-permute-start(bf16[4,24,2432]{2,1,0:T(8,128)(2,1)} %bitcast.40), channel_id=1, source_target_pairs={{0,1},{1,0},{2,3},{3,2},{4,5},{5,4},{6,7},{7,6},{8,9},{9,8},{10,11... | collective-permute-start | bytes 1400840 | tf_op jit(solution)/shard_map/ppermute | solution.py:620
  593.6 11.1 %collective-permute-start.10 = (bf16[1,24,3840]{2,1,0:T(8,128)(2,1)S(1)}, bf16[1,24,3840]{2,1,0:T(8,128)(2,1)S(1)}, u32[]{:S(2)}, u32[]{:S(2)}) collective-permute-start(bf16[1,24,3840]{2,1,0:T(8,128)(2,1)S(1)} %bitcast.89), channel_id=1, source_target_pairs={{0,4},{1,5},{2,6},{3,7},{4,0},{5,1},{6,2},{7,3},{8,12},{9,13},{10,... | collective-permute-start | bytes 552968 | tf_op jit(solution)/shard_map/ppermute | solution.py:620
  598.3 9.6 %collective-permute-start.13 = (bf16[2,24,2432]{2,1,0:T(8,128)(2,1)S(1)}, bf16[2,24,2432]{2,1,0:T(8,128)(2,1)S(1)}, u32[]{:S(2)}, u32[]{:S(2)}) collective-permute-start(bf16[2,24,2432]{2,1,0:T(8,128)(2,1)S(1)} %bitcast.88), channel_id=1, source_target_pairs={{0,2},{1,3},{2,0},{3,1},{4,6},{5,7},{6,4},{7,5},{8,10},{9,11},{10,... | collective-permute-start | bytes 700424 | tf_op jit(solution)/shard_map/ppermute | solution.py:620
  608.0 12.8 %collective-permute-start.14 = (bf16[1,24,2432]{2,1,0:T(8,128)(2,1)S(1)}, bf16[1,24,2432]{2,1,0:T(8,128)(2,1)S(1)}, u32[]{:S(2)}, u32[]{:S(2)}) collective-permute-start(bf16[1,24,2432]{2,1,0:T(8,128)(2,1)S(1)} %bitcast.90), channel_id=1, source_target_pairs={{0,4},{1,5},{2,6},{3,7},{4,0},{5,1},{6,2},{7,3},{8,12},{9,13},{10,... | collective-permute-start | bytes 350216 | tf_op jit(solution)/shard_map/ppermute | solution.py:620
  (72 other events, 244.0 us)
Sparse Core Ops, SparseCore 0:
  13.1 81.3 all-gather.2
  98.0 121.0 all-gather.4
  356.1 216.6 reduce-scatter.1
where the time goes:
time: 643 us; the launch traced here: 632 us
  Pallas kernels  297 us (46%)
  waiting for transfers between devices  139 us (22%)
  starting transfers between devices  98.2 us (15%)
  local copies, waits for them, and re-layouts  78.8 us (12%)
  between operations  14.9 us (2%)
    ppermute x15, waiting for transfers between devices, swap(): lax.ppermute(array, axis, [(i, i ^ 1 << b) for i in range(lax.axis_size(a...  123 us
    unnamed x194, local copies, waits for them, and re-layouts  59.6 us
    pallas_call x2, Pallas kernels, run_cross_backward(): pl.pallas_call(cross_backward_kernel, name='cross_backward', grid=(PAIRS,...  59 us
    ppermute x15, starting transfers between devices, swap(): lax.ppermute(array, axis, [(i, i ^ 1 << b) for i in range(lax.axis_size(a...  51 us
    all_to_all x7, starting transfers between devices, exchange(): lax.all_to_all(array, 'fsdp', split_axis=0, concat_axis=0, tiled=True)  47.1 us
    pallas_call x2, Pallas kernels, run_middle(): pl.pallas_call(middle_kernel, name='mlp_and_back', grid_spec=pltpu.Prefet...  41.4 us
    pallas_call x2, Pallas kernels, run_cross_forward(): pl.pallas_call(cross_forward_kernel, name='cross_forward', grid=(PAIRS,),...  39.8 us
    pallas_call x5, Pallas kernels, run_grad(): pl.pallas_call(functools.partial(grad_kernel, full), name=name, grid=(wid...  37.5 us
  transfers between devices with their start and end apart: 25, of which 14 were waited for; matrix products, arithmetic and copies ran while one was open for 4% of the time, Pallas kernels for 47%

commit v1 on v0

--- a/solution.py
+++ b/solution.py
@@ -1094,33 +1094,35 @@
     (back_a, cb0, cb1, mid0, mid1) = fence(back_a, cb0, cb1, mid0, mid1)
 
     back_b = exchange(cb1[2])
+    halves = run_grad("grad_cross_kv", lens, ((in_a, cb0[1]), (in_c, cb1[1])), 3 * D, 0, full=True)
+    halves = run_grad(
+        "grad_cross_out", lens, ((crs0[0], mid0[4]), (crs1[0], mid1[4])), 3 * D, 2, halves
+    )
+    g_two = Scatter("two", *halves)
+    g_two.step()
+    (g_two.keep, g_two.send, cb0, cb1) = fence(g_two.keep, g_two.send, cb0, cb1)
+    g_two.move()
     sb0 = run_self_backward(
         len0, cb0[0], mid0[5], fwd0[4], fwd0[0], fwd0[2], fwd0[3], in_t, "first", w_one, norm_rows, None, 0
     )
     sb1 = run_self_backward(
         len1, cb1[0], mid1[5], fwd1[4], fwd1[0], fwd1[2], fwd1[3], in_t, "second", w_one, norm_rows, sb0[2], 1
     )
-    halves = run_grad("grad_self_in", lens, ((fwd0[1], sb0[1]), (fwd1[1], sb1[1])), 5 * D, 0)
-    halves = run_grad("grad_self_out", lens, ((fwd0[2], sb0[0]), (fwd1[2], sb1[0])), 5 * D, 3, halves)
-    halves = run_grad("grad_cross_q", lens, ((fwd0[5], cb0[0]), (fwd1[5], cb1[0])), 5 * D, 4, halves)
-    g_one = Scatter("one", *halves)
-    gtok, sb0, sb1 = sb1[2], (sb0[0], sb0[1], sb0[3]), (sb1[0], sb1[1], sb1[3])
-    (sb0, sb1, g_one.keep, g_one.send, cb0, cb1, mid0, mid1) = fence(
-        sb0, sb1, g_one.keep, g_one.send, cb0, cb1, mid0, mid1
-    )
-    g_one.step()
-    halves = run_grad("grad_cross_kv", lens, ((in_a, cb0[1]), (in_c, cb1[1])), 3 * D + PAIR, 0, full=True)
-    (g_one.keep, g_one.send, halves, cb0, cb1) = fence(g_one.keep, g_one.send, halves, cb0, cb1)
-    g_one.move()
-    halves = run_grad(
-        "grad_cross_out", lens, ((crs0[0], mid0[4]), (crs1[0], mid1[4])), 3 * D + PAIR, 2, halves
-    )
-    ng_self = sb0[2] + sb1[2]
+    sb0 = (sb0[0], sb0[1], sb1[2], sb0[3])
+    (sb0, sb1, g_two.got) = fence(sb0, sb1, g_two.got)
+    g_two.take()
+    halves = run_grad("grad_self_in", lens, ((fwd0[1], sb0[1]), (fwd1[1], sb1[1])), 5 * D + PAIR, 0)
+    halves = run_grad("grad_self_out", lens, ((fwd0[2], sb0[0]), (fwd1[2], sb1[0])), 5 * D + PAIR, 3, halves)
+    halves = run_grad("grad_cross_q", lens, ((fwd0[5], cb0[0]), (fwd1[5], cb1[0])), 5 * D + PAIR, 4, halves)
+    ng_self = sb0[3] + sb1[3]
     ng_mid = mid0[7] + mid1[7]
     norm_sum = jnp.concatenate([ng_self[:2], ng_mid[:2], ng_self[2:4], ng_mid[2:4]], axis=0)
-    g_two = Scatter("two", *put_norm_grad(norm_sum, halves))
+    g_one = Scatter("one", *put_norm_grad(norm_sum, halves))
+    gtok = sb1[2]
+    g_one.step()
+    (g_one.keep, g_one.send, back_b, gtok) = fence(g_one.keep, g_one.send, back_b, gtok)
+    g_one.move()
     g_two.move()
-    (back_b, g_two.got, gtok) = fence(back_b, g_two.got, gtok)
 
     back_c = exchange(gtok)
     grad_frames, output = put_back(
@@ -1130,7 +1132,7 @@
     )
     g_one = g_one.finish()
     g_two = g_two.finish()
-    g_norm = g_two[:, 3 * D : 3 * D + 8]
+    g_norm = g_one[:, 5 * D : 5 * D + 8]
     (grad_tokens,) = put_back("put_tokens", (back_c, slice(0, size), back_c, slice(size, 2 * size)))
     return (
         output,
@@ -1138,9 +1140,9 @@
         grad_frames,
         by_part(g_one[:, :ONE_OUT], 3),
         g_one[:, ONE_OUT:ONE_Q],
-        g_one[:, ONE_Q:],
+        g_one[:, ONE_Q:ONE_NORM],
         by_part(g_two[:, :TWO_OUT], 2),
-        g_two[:, TWO_OUT : 3 * D],
+        g_two[:, TWO_OUT:],
         g_fc[:, :FF].astype(f32).reshape(rows, FF_PARTS, n_all, rows).swapaxes(1, 2).reshape(rows, FF),
         g_fc[:, FF:].astype(f32).reshape(rows, FF_PARTS, D).swapaxes(0, 1).reshape(FF_PARTS * rows, D),
         g_norm[:, :4],

time: 643 us -> 664 us (1.033)
  waiting for transfers between devices: 139 us -> 180 us
  starting transfers between devices: 98.2 us -> 89.3 us
    ppermute x15, starting transfers between devices: 51 us -> 22.3 us  [swap(): lax.ppermute(array, axis, [(i, i ^ 1 << b) for i in range(lax.axis_size(a...]
    all_to_all x7, waiting for transfers between devices: 16.2 us -> 37.3 us  [exchange(): lax.all_to_all(array, 'fsdp', split_axis=0, concat_axis=0, tiled=True)]
    ppermute x15, waiting for transfers between devices: 123 us -> 143 us  [swap(): lax.ppermute(array, axis, [(i, i ^ 1 << b) for i in range(lax.axis_size(a...]
    all_to_all x7, starting transfers between devices: 47.1 us -> 66.9 us  [exchange(): lax.all_to_all(array, 'fsdp', split_axis=0, concat_axis=0, tiled=True)]
    unnamed x194 -> x184, local copies, waits for them, and re-layouts: 59.6 us -> 53.2 us
  transfers between devices with their start and end apart: 25 -> 25, of which waited for: 14 -> 15; matrix products, arithmetic and copies ran while one was open for 4% -> 3% of each run, Pallas kernels for 47% -> 45%
where the time goes in v1:
time: 664 us; the launch traced here: 657 us
  Pallas kernels  295 us (44%)
  waiting for transfers between devices  180 us (27%)
  starting transfers between devices  89.3 us (13%)
  local copies, waits for them, and re-layouts  72.4 us (11%)
  between operations  15.2 us (2%)
    ppermute x15, waiting for transfers between devices, swap(): lax.ppermute(array, axis, [(i, i ^ 1 << b) for i in range(lax.axis_size(a...  143 us
    all_to_all x7, starting transfers between devices, exchange(): lax.all_to_all(array, 'fsdp', split_axis=0, concat_axis=0, tiled=True)  66.9 us
    pallas_call x2, Pallas kernels, run_cross_backward(): pl.pallas_call(cross_backward_kernel, name='cross_backward', grid=(PAIRS,...  58.8 us
    unnamed x184, local copies, waits for them, and re-layouts  53.2 us
    pallas_call x2, Pallas kernels, run_middle(): pl.pallas_call(middle_kernel, name='mlp_and_back', grid_spec=pltpu.Prefet...  41.4 us
    pallas_call x2, Pallas kernels, run_cross_forward(): pl.pallas_call(cross_forward_kernel, name='cross_forward', grid=(PAIRS,),...  39.5 us
    pallas_call x5, Pallas kernels, run_grad(): pl.pallas_call(functools.partial(grad_kernel, full), name=name, grid=(wid...  38 us
    all_to_all x7, waiting for transfers between devices, exchange(): lax.all_to_all(array, 'fsdp', split_axis=0, concat_axis=0, tiled=True)  37.3 us
  transfers between devices with their start and end apart: 25, of which 15 were waited for; matrix products, arithmetic and copies ran while one was open for 3% of the time, Pallas kernels for 45%

profile of v1, /device:TPU:0, one launch (start us, length us, event | category | flops | bytes accessed | tf_op | source)
XLA Modules:
  0.0 657.3 jit_solution(14205183845817999435)
XLA Ops:
  13.0 4.1 collective-permute-start
  20.7 3.7 pick_tokens.1
  31.6 10.0 %collective-permute-done.1.refs_1_ = bf16[2,24,3968]{2,1,0:T(8,128)(2,1)S(1)} collective-permute-done((bf16[2,24,3968]{2,1,0:T(8,128)(2,1)S(1)}, bf16[2,24,3968]{2,1,0:T(8,128)(2,1)S(1)}, u32[]{:S(2)}, u32[]{:S(2)}) %collective-permute-start.1) | collective-permute-done | bytes 380960 | tf_op jit(solution)/shard_map/ppermute | solution.py:620
  42.4 6.1 all-to-all-start
  55.4 34.4 %collective-permute-done.2.refs_1_ = bf16[4,24,3968]{2,1,0:T(8,128)(2,1)S(1)} collective-permute-done((bf16[4,24,3968]{2,1,0:T(8,128)(2,1)S(1)}, bf16[4,24,3968]{2,1,0:T(8,128)(2,1)S(1)}, u32[]{:S(2)}, u32[]{:S(2)}) %collective-permute-start.2) | collective-permute-done | bytes 761888 | tf_op jit(solution)/shard_map/ppermute | solution.py:620
  90.9 4.9 all-to-all-done.tok_ref.refs_7_
  97.2 4.4 all-to-all-start.1
  103.9 3.7 pick_third.1
  110.2 22.5 %collective-permute-done.3.refs_1_ = bf16[8,24,3968]{2,1,0:T(8,128)(2,1)} collective-permute-done((bf16[8,24,3968]{2,1,0:T(8,128)(2,1)}, bf16[8,24,3968]{2,1,0:T(8,128)(2,1)}, u32[]{:S(2)}, u32[]{:S(2)}) %collective-permute-start.3) | collective-permute-done | bytes 1523744 | tf_op jit(solution)/shard_map/ppermute | solution.py:620
  132.6 3.0 one_join.7.refs_0_
  137.1 4.5 collective-permute-done.4.refs_1_
  143.7 4.4 one_order.1
  149.2 2.7 copy-done
  152.0 7.9 %self_part_forward.3 = (bf16[512,2304]{1,0:T(8,128)(2,1)}, bf16[512,768]{1,0:T(8,128)(2,1)}, bf16[512,768]{1,0:T(8,128)(2,1)}, f32[6,4,256]{2,1,0:T(4,128)}, f32...) custom-call(s32[1]{0:T(128)} %get-tuple-element.426.len_ref.len1_ref, ...), custom_call_target="tpu_custom_call" | custom-call | flops 1000000 | bytes 1000000 | tf_op jit(solution)/shard_map/self_part_forward/pallas_call | solution.py:215
  159.8 18.3 %self_part_forward.2 = (bf16[512,2304]{1,0:T(8,128)(2,1)}, bf16[512,768]{1,0:T(8,128)(2,1)}, bf16[512,768]{1,0:T(8,128)(2,1)}, f32[6,4,256]{2,1,0:T(4,128)}, f32...) custom-call(s32[1]{0:T(128)} %get-tuple-element.427.len_ref.len0_ref.refs_0_, ...), custom_call_target="tpu_custom_call" | custom-call | flops 1000000 | bytes 1000000 | tf_op jit(solution)/shard_map/self_part_forward/pallas_call | solution.py:215
  178.2 3.5 all-to-all-start.2
  184.9 23.8 %cross_forward.2 = (bf16[512,768]{1,0:T(8,128)(2,1)}, f32[6,2,512]{2,1,0:T(2,128)}, bf16[1536,1536]{1,0:T(8,128)(2,1)}) custom-call(s32[1]{0:T(128)} %get-tuple-element.427.len_ref.len0_ref.refs_0_, bf16[8,192,768]{2,1,0:T(8,128)(2,1)} %all-to-all-done.1.frm_ref.left0_ref, bf16[768,2304]{1,0:T(8,128)(2,1)S(1)} %copy-done.1, bf16[512,768]{1,0:T(8,128)(2,1)S(1)} %copy-done.39), custom_call_target="tpu_custom_call" | custom-call | flops 1000000 | bytes 1000000 | tf_op jit(solution)/shard_map/cross_forward/pallas_call | solution.py:271
  208.7 5.7 all-to-all-done.2.cot_ref
  215.3 6.0 all-to-all-start.3
  225.9 24.6 %mlp_and_back.2 = (bf16[8,256,768]{2,1,0:T(8,128)(2,1)}, bf16[512,768]{1,0:T(8,128)(2,1)}, bf16[512,3072]{1,0:T(8,128)(2,1)}, bf16[512,3072]{1,0:T(8,128)(2,1)},...) custom-call(s32[1]{0:T(128)} %get-tuple-element.427.len_ref.len0_ref, ...), custom_call_target="tpu_custom_call" | custom-call | flops 1000000 | bytes 1000000 | tf_op jit(solution)/shard_map/mlp_and_back/pallas_call | solution.py:452
  251.6 36.7 %cross_backward.2 = (bf16[512,768]{1,0:T(8,128)(2,1)}, bf16[1536,1536]{1,0:T(8,128)(2,1)}, bf16[8,256,768]{2,1,0:T(8,128)(2,1)}) custom-call(s32[1]{0:T(128)} %get-tuple-element.427.len_ref.len0_ref.refs_0_, bf16[512,768]{1,0:T(8,128)(2,1)S(1)} %copy-done.40, bf16[1536,1536]{1,0:T(8,128)(2,1)S(1)} %copy-done.24, ...), custom_call_target="tpu_custom_call", output_to_operand_aliasing={{2}: (7, {})} | custom-call | flops 1000000 | bytes 1000000 | tf_op jit(solution)/shard_map/cross_backward/pallas_call | solution.py:348
  288.3 5.2 all-to-all-done.3.frm_ref.cot_ref.left1_ref
  293.6 4.4 all-to-all-start.4
  299.2 15.7 %cross_forward.3 = (bf16[512,768]{1,0:T(8,128)(2,1)}, f32[6,2,512]{2,1,0:T(2,128)}, bf16[1536,1536]{1,0:T(8,128)(2,1)}) custom-call(s32[1]{0:T(128)} %get-tuple-element.426.len_ref.len1_ref, bf16[8,256,768]{2,1,0:T(8,128)(2,1)} %all-to-all-done.3.frm_ref.cot_ref.left1_ref, bf16[768,2304]{1,0:T(8,128)(2,1)S(1)} %copy-done.2, bf16[512,768]{1,0:T(8,128)(2,1)S(1)} %copy-done.37), custom_call_target="tpu_custom_call" | custom-call | flops 1000000 | bytes 1000000 | tf_op jit(solution)/shard_map/cross_forward/pallas_call | solution.py:271
  316.1 16.8 %mlp_and_back.3 = (bf16[8,256,768]{2,1,0:T(8,128)(2,1)}, bf16[512,768]{1,0:T(8,128)(2,1)}, bf16[512,3072]{1,0:T(8,128)(2,1)}, bf16[512,3072]{1,0:T(8,128)(2,1)},...) custom-call(s32[1]{0:T(128)} %get-tuple-element.426.len_ref.len1_ref, ...), custom_call_target="tpu_custom_call" | custom-call | flops 1000000 | bytes 1000000 | tf_op jit(solution)/shard_map/mlp_and_back/pallas_call | solution.py:452
  339.0 17.5 %grad_fc.1 = bf16[768,6144]{1,0:T(8,128)(2,1)} custom-call(s32[1]{0:T(128)} %get-tuple-element.427.len_ref.len0_ref.refs_0_, s32[1]{0:T(128)} %get-tuple-element.426.len_ref.len1_ref, bf16[512,768]{1,0:T(8,128)(2,1)S(1)} %copy-done.56, bf16[512,3072]{1,0:T(8,128)(2,1)S(1)} %copy-done.34, bf16[512,3072]{1,0:T(8,128)(2,1)S(1)} %copy-done.33, ...), custom_call_target="tpu_custom_call" | custom-call | flops 1000000 | bytes 1000000 | tf_op jit(solution)/shard_map/grad_fc/pallas_call | solution.py:836
  365.0 22.1 %cross_backward.3 = (bf16[512,768]{1,0:T(8,128)(2,1)}, bf16[1536,1536]{1,0:T(8,128)(2,1)}, bf16[8,256,768]{2,1,0:T(8,128)(2,1)}) custom-call(s32[1]{0:T(128)} %get-tuple-element.426.len_ref.len1_ref, bf16[512,768]{1,0:T(8,128)(2,1)S(1)} %copy-done.38, bf16[1536,1536]{1,0:T(8,128)(2,1)S(1)} %copy-done.23, ...), custom_call_target="tpu_custom_call", output_to_operand_aliasing={{2}: (7, {})} | custom-call | flops 1000000 | bytes 1000000 | tf_op jit(solution)/shard_map/cross_backward/pallas_call | solution.py:348
  387.2 16.4 %grad_cross_kv.1 = (bf16[2,192,2304]{2,1,0:T(8,128)(2,1)}, bf16[2,192,2304]{2,1,0:T(8,128)(2,1)}) custom-call(s32[1]{0:T(128)} %get-tuple-element.427.len_ref.len0_ref.refs_0_, s32[1]{0:T(128)} %get-tuple-element.426.len_ref.len1_ref, s32[1]{0:T(128)} %bitcast.11.bit_ref, bf16[8,192,768]{2,1,0:T(8,128)(2,1)} %all-to-all-done.1.frm_ref.left0_ref, ...), custom_call_target="tpu_custom_call" | custom-call | flops 1000000 | bytes 1000000 | tf_op jit(solution)/shard_map/grad_cross_kv/pallas_call | solution.py:864
  403.6 4.3 grad_cross_out.1
  408.0 38.9 %all-to-all-start.5 = ((bf16[8,256,768]{2,1,0:T(8,128)(2,1)}), bf16[8,256,768]{2,1,0:T(8,128)(2,1)}, u32[]{:S(2)}, u32[]{:S(2)}) async-start(bf16[8,256,768]{2,1,0:T(8,128)(2,1)} %get-tuple-element.316), calls=%async_computation.5 | async-start | bytes 6291456 | tf_op jit(solution)/shard_map/all_to_all | solution.py:972
  458.0 20.7 %self_part_backward.2 = (bf16[512,768]{1,0:T(8,128)(2,1)}, bf16[512,2304]{1,0:T(8,128)(2,1)}, bf16[8,128,768]{2,1,0:T(8,128)(2,1)}, f32[8,768]{1,0:T(8,128)}) custom-call(s32[1]{0:T(128)} %get-tuple-element.427.len_ref.len0_ref.refs_0_, bf16[512,768]{1,0:T(8,128)(2,1)S(1)} %copy-done.28, f32[512,768]{1,0:T(8,128)S(1)} %copy-done.45, ...), custom_call_target="tpu_custom_call" | custom-call | flops 1000000 | bytes 1000000 | tf_op jit(solution)/shard_map/self_part_backward/pallas_call | solution.py:557
  478.7 10.9 %self_part_backward.3 = (bf16[512,768]{1,0:T(8,128)(2,1)}, bf16[512,2304]{1,0:T(8,128)(2,1)}, bf16[8,128,768]{2,1,0:T(8,128)(2,1)}, f32[8,768]{1,0:T(8,128)}) custom-call(s32[1]{0:T(128)} %get-tuple-element.426.len_ref.len1_ref, bf16[512,768]{1,0:T(8,128)(2,1)S(1)} %copy-done.30, f32[512,768]{1,0:T(8,128)S(1)} %copy-done.46, ...), custom_call_target="tpu_custom_call", output_to_operand_aliasing={{2}: (10, {})} | custom-call | flops 1000000 | bytes 1000000 | tf_op jit(solution)/shard_map/self_part_backward/pallas_call | solution.py:557
  490.4 8.5 %grad_self_in.1 = (bf16[2,192,3968]{2,1,0:T(8,128)(2,1)}, bf16[2,192,3968]{2,1,0:T(8,128)(2,1)}) custom-call(s32[1]{0:T(128)} %get-tuple-element.427.len_ref.len0_ref.refs_0_, s32[1]{0:T(128)} %get-tuple-element.426.len_ref.len1_ref, s32[1]{0:T(128)} %bitcast.11.bit_ref, bf16[512,768]{1,0:T(8,128)(2,1)S(1)} %copy-done.67, bf16[512,2304]{1,0:T(8,128)(2,1)S(1)} %copy-done.43, ...), custom_call_target="tpu_custom_call" | custom-call | flops 1000000 | bytes 1000000 | tf_op jit(solution)/shard_map/grad_self_in/pallas_call | solution.py:864
  499.0 4.4 grad_self_out.1
  503.4 4.5 grad_cross_q.1
  508.8 5.7 collective-permute-done.7
  518.4 21.5 %all-to-all-done.5.refs_1_ = bf16[8,256,768]{2,1,0:T(8,128)(2,1)} async-done(((bf16[8,256,768]{2,1,0:T(8,128)(2,1)}), bf16[8,256,768]{2,1,0:T(8,128)(2,1)}, u32[]{:S(2)}, u32[]{:S(2)}) %all-to-all-start.5) | async-done | bytes 3145760 | tf_op jit(solution)/shard_map/all_to_all | solution.py:972
  541.9 3.6 all-to-all-start.6
  545.5 32.0 %collective-permute-done.8 = bf16[8,24,3968]{2,1,0:T(8,128)(2,1)} collective-permute-done((bf16[8,24,3968]{2,1,0:T(8,128)(2,1)}, bf16[8,24,3968]{2,1,0:T(8,128)(2,1)}, u32[]{:S(2)}, u32[]{:S(2)}) %collective-permute-start.8) | collective-permute-done | bytes 1523744 | tf_op jit(solution)/shard_map/ppermute | solution.py:620
  577.5 3.5 one_add.5
  584.4 16.7 %collective-permute-done.9 = bf16[4,24,3968]{2,1,0:T(8,128)(2,1)S(1)} collective-permute-done((bf16[4,24,3968]{2,1,0:T(8,128)(2,1)}, bf16[4,24,3968]{2,1,0:T(8,128)(2,1)S(1)}, u32[]{:S(2)}, u32[]{:S(2)}) %collective-permute-start.9) | collective-permute-done | bytes 761888 | tf_op jit(solution)/shard_map/ppermute | solution.py:620
  605.0 4.2 collective-permute-done.12
  610.5 7.2 %collective-permute-done.13 = bf16[2,24,2304]{2,1,0:T(8,128)(2,1)S(1)} collective-permute-done((bf16[2,24,2304]{2,1,0:T(8,128)(2,1)S(1)}, bf16[2,24,2304]{2,1,0:T(8,128)(2,1)S(1)}, u32[]{:S(2)}, u32[]{:S(2)}) %collective-permute-start.13) | collective-permute-done | bytes 221216 | tf_op jit(solution)/shard_map/ppermute | solution.py:620
  617.8 2.8 collective-permute-start.14
  620.6 4.1 collective-permute-done.14.got_ref
  626.2 5.5 put_frames.1
  636.9 3.8 copy.68
  640.7 4.0 reshape.307
  (269 shorter events, 102.2 us)
Async XLA Ops:
  7.2 174.6 %all-gather.3.cloned.1.call-start = ((), (), s32[]{:S(2)}) async-start(), calls=%async_computation.8 | async-start | bytes 3649536 | tf_op jit(solution)/shard_map/all_gather | solution.py:706
  13.0 208.3 %all-gather.5.cloned.1.call-start = ((), (), s32[]{:S(2)}) async-start(), calls=%async_computation.9 | async-start | bytes 9732096 | tf_op jit(solution)/shard_map/all_gather | solution.py:706
  13.0 13.2 %collective-permute-start = (bf16[1,24,3968]{2,1,0:T(8,128)(2,1)}, bf16[1,24,3968]{2,1,0:T(8,128)(2,1)S(1)}, u32[]{:S(2)}, u32[]{:S(2)}) collective-permute-start(bf16[1,24,3968]{2,1,0:T(8,128)(2,1)} %bitcast.85), channel_id=1, source_target_pairs={{0,4},{1,5},{2,6},{3,7},{4,0},{5,1},{6,2},{7,3},{8,12},{9,13},{10,... | collective-permute-start | bytes 571400 | tf_op jit(solution)/shard_map/ppermute | solution.py:620
  30.5 11.0 %collective-permute-start.1 = (bf16[2,24,3968]{2,1,0:T(8,128)(2,1)S(1)}, bf16[2,24,3968]{2,1,0:T(8,128)(2,1)S(1)}, u32[]{:S(2)}, u32[]{:S(2)}) collective-permute-start(bf16[2,24,3968]{2,1,0:T(8,128)(2,1)S(1)} %copy-done.47), channel_id=1, source_target_pairs={{0,2},{1,3},{2,0},{3,1},{4,6},{5,7},{6,4},{7,5},{8,10},{9,11},{10,... | collective-permute-start | bytes 1142792 | tf_op jit(solution)/shard_map/ppermute | solution.py:620
  42.4 53.4 %all-to-all-start = ((bf16[8,128,768]{2,1,0:T(8,128)(2,1)}), bf16[8,128,768]{2,1,0:T(8,128)(2,1)S(1)}, u32[]{:S(2)}, u32[]{:S(2)}) async-start(bf16[8,128,768]{2,1,0:T(8,128)(2,1)} %pick_tokens.1), calls=%async_computation | async-start | bytes 3145728 | tf_op jit(solution)/shard_map/all_to_all | solution.py:972
  48.5 41.2 %collective-permute-start.2 = (bf16[4,24,3968]{2,1,0:T(8,128)(2,1)S(1)}, bf16[4,24,3968]{2,1,0:T(8,128)(2,1)S(1)}, u32[]{:S(2)}, u32[]{:S(2)}) collective-permute-start(bf16[4,24,3968]{2,1,0:T(8,128)(2,1)S(1)} %copy-done.41), channel_id=1, source_target_pairs={{0,1},{1,0},{2,3},{3,2},{4,5},{5,4},{6,7},{7,6},{8,9},{9,8},{10,11... | collective-permute-start | bytes 2285576 | tf_op jit(solution)/shard_map/ppermute | solution.py:620
  95.8 64.0 %copy-start.5 = (bf16[8,128,768]{2,1,0:T(8,128)(2,1)}, bf16[8,128,768]{2,1,0:T(8,128)(2,1)S(1)}, u32[]{:S(2)}) copy-start(bf16[8,128,768]{2,1,0:T(8,128)(2,1)S(1)} %all-to-all-done.tok_ref.refs_7_) | copy-start | bytes 4718596
  95.8 36.8 %collective-permute-start.3 = (bf16[8,24,3968]{2,1,0:T(8,128)(2,1)}, bf16[8,24,3968]{2,1,0:T(8,128)(2,1)}, u32[]{:S(2)}, u32[]{:S(2)}) collective-permute-start(bf16[8,24,3968]{2,1,0:T(8,128)(2,1)} %one_join.6.refs_0_), channel_id=1, source_target_pairs={{0,16},{8,24},{16,0},{24,8},{1,17},{9,25},{17,1},{25,9},{2,18},{10... | collective-permute-start | bytes 4571144 | tf_op jit(solution)/shard_map/ppermute | solution.py:620
  97.2 81.0 %all-to-all-start.1 = ((bf16[8,192,768]{2,1,0:T(8,128)(2,1)}), bf16[8,192,768]{2,1,0:T(8,128)(2,1)}, u32[]{:S(2)}, u32[]{:S(2)}) async-start(bf16[8,192,768]{2,1,0:T(8,128)(2,1)} %pick_frames.1), calls=%async_computation.1 | async-start | bytes 4718592 | tf_op jit(solution)/shard_map/all_to_all | solution.py:972
  107.6 25.0 %copy-start.22 = (bf16[8,24,3968]{2,1,0:T(8,128)(2,1)S(1)}, bf16[8,24,3968]{2,1,0:T(8,128)(2,1)}, u32[]{:S(2)}) copy-start(bf16[8,24,3968]{2,1,0:T(8,128)(2,1)} %one_join.6.refs_0_) | copy-start | bytes 4571140
  110.1 25.7 %copy-start.84 = (s32[16]{0:T(128)S(1)}, s32[16]{0:T(128)}, u32[]{:S(2)}) copy-start(s32[16]{0:T(128)} %param.15) | copy-start | bytes 196
  135.7 5.9 collective-permute-start.4
  178.2 36.2 %all-to-all-start.2 = ((bf16[8,64,768]{2,1,0:T(8,128)(2,1)}), bf16[8,64,768]{2,1,0:T(8,128)(2,1)S(1)}, u32[]{:S(2)}, u32[]{:S(2)}) async-start(bf16[8,64,768]{2,1,0:T(8,128)(2,1)} %pick_cotangent.1), calls=%async_computation.2 | async-start | bytes 1572864 | tf_op jit(solution)/shard_map/all_to_all | solution.py:972
  215.3 78.3 %all-to-all-start.3 = ((bf16[8,256,768]{2,1,0:T(8,128)(2,1)}), bf16[8,256,768]{2,1,0:T(8,128)(2,1)}, u32[]{:S(2)}, u32[]{:S(2)}) async-start(bf16[8,256,768]{2,1,0:T(8,128)(2,1)} %pick_third.1), calls=%async_computation.3 | async-start | bytes 6291456 | tf_op jit(solution)/shard_map/all_to_all | solution.py:972
  221.3 29.2 %copy-start.2 = (bf16[768,2304]{1,0:T(8,128)(2,1)S(1)}, bf16[768,2304]{1,0:T(8,128)(2,1)}, u32[]{:S(2)}) copy-start(bf16[768,2304]{1,0:T(8,128)(2,1)} %all-gather.3.cloned.1.call-done.w_ref.two_ref) | copy-start | bytes 10616836
  225.9 24.6 %copy-start.24 = (bf16[1536,1536]{1,0:T(8,128)(2,1)S(1)}, bf16[1536,1536]{1,0:T(8,128)(2,1)}, u32[]{:S(2)}) copy-start(bf16[1536,1536]{1,0:T(8,128)(2,1)} %get-tuple-element.241.kv_ref) | copy-start | bytes 14155780
  225.9 24.6 %copy-start.40 = (bf16[512,768]{1,0:T(8,128)(2,1)S(1)}, bf16[512,768]{1,0:T(8,128)(2,1)}, u32[]{:S(2)}) copy-start(bf16[512,768]{1,0:T(8,128)(2,1)} %get-tuple-element.242.q_ref) | copy-start | bytes 2359300
  225.9 24.6 %copy-start.82 = (f32[6,2,512]{2,1,0:T(2,128)S(1)}, f32[6,2,512]{2,1,0:T(2,128)}, u32[]{:S(2)}) copy-start(f32[6,2,512]{2,1,0:T(2,128)} %get-tuple-element.240.lse_ref) | copy-start | bytes 73732
  293.6 93.6 %all-to-all-start.4 = ((bf16[8,256,768]{2,1,0:T(8,128)(2,1)}), bf16[8,256,768]{2,1,0:T(8,128)(2,1)}, u32[]{:S(2)}, u32[]{:S(2)}) async-start(bf16[8,256,768]{2,1,0:T(8,128)(2,1)} %get-tuple-element.266), calls=%async_computation.4 | async-start | bytes 6291456 | tf_op jit(solution)/shard_map/all_to_all | solution.py:972
  298.0 335.5 %reduce-scatter.2.cloned.1.call-start = ((), (), s32[]{:S(2)}) async-start(), calls=%async_computation.10 | async-start | bytes 9732096 | tf_op jit(solution)/shard_map/reduce_scatter | solution.py:1092
  316.1 16.8 %copy-start.33 = (bf16[512,3072]{1,0:T(8,128)(2,1)S(1)}, bf16[512,3072]{1,0:T(8,128)(2,1)}, u32[]{:S(2)}) copy-start(bf16[512,3072]{1,0:T(8,128)(2,1)} %get-tuple-element.285.hid0_ref) | copy-start | bytes 9437188
  316.1 16.8 %copy-start.34 = (bf16[512,3072]{1,0:T(8,128)(2,1)S(1)}, bf16[512,3072]{1,0:T(8,128)(2,1)}, u32[]{:S(2)}) copy-start(bf16[512,3072]{1,0:T(8,128)(2,1)} %get-tuple-element.284.pre0_ref) | copy-start | bytes 9437188
  316.1 16.9 %copy-start.56 = (bf16[512,768]{1,0:T(8,128)(2,1)S(1)}, bf16[512,768]{1,0:T(8,128)(2,1)}, u32[]{:S(2)}) copy-start(bf16[512,768]{1,0:T(8,128)(2,1)} %get-tuple-element.283.normed0_ref) | copy-start | bytes 2359300
  316.1 16.9 %copy-start.57 = (bf16[512,768]{1,0:T(8,128)(2,1)S(1)}, bf16[512,768]{1,0:T(8,128)(2,1)}, u32[]{:S(2)}) copy-start(bf16[512,768]{1,0:T(8,128)(2,1)} %get-tuple-element.286.branch0_ref) | copy-start | bytes 2359300
  387.1 16.4 %copy-start.11 = (bf16[512,768]{1,0:T(8,128)(2,1)S(1)}, bf16[512,768]{1,0:T(8,128)(2,1)}, u32[]{:S(2)}) copy-start(bf16[512,768]{1,0:T(8,128)(2,1)} %get-tuple-element.303.mix_ref.left0_ref) | copy-start | bytes 2359300
  387.2 16.4 %copy-start.14 = (bf16[512,768]{1,0:T(8,128)(2,1)S(1)}, bf16[512,768]{1,0:T(8,128)(2,1)}, u32[]{:S(2)}) copy-start(bf16[512,768]{1,0:T(8,128)(2,1)} %get-tuple-element.289.mix_ref.left1_ref) | copy-start | bytes 2359300
  387.2 16.4 %copy-start.68 = (bf16[512,768]{1,0:T(8,128)(2,1)S(1)}, bf16[512,768]{1,0:T(8,128)(2,1)}, u32[]{:S(2)}) copy-start(bf16[512,768]{1,0:T(8,128)(2,1)} %get-tuple-element.304.right0_ref) | copy-start | bytes 2359300
  407.9 39.1 %copy-start.15 = (bf16[2,192,2304]{2,1,0:T(8,128)(2,1)S(1)}, bf16[2,192,2304]{2,1,0:T(8,128)(2,1)}, u32[]{:S(2)}) copy-start(bf16[2,192,2304]{2,1,0:T(8,128)(2,1)} %get-tuple-element.310) | copy-start | bytes 5308420
  407.9 39.1 %collective-permute-start.5 = (bf16[16,24,2304]{2,1,0:T(8,128)(2,1)}, bf16[16,24,2304]{2,1,0:T(8,128)(2,1)}, u32[]{:S(2)}, u32[]{:S(2)}) collective-permute-start(bf16[16,24,2304]{2,1,0:T(8,128)(2,1)} %bitcast.96), channel_id=1, source_target_pairs={{0,8},{8,0},{16,24},{24,16},{1,9},{9,1},{17,25},{25,17},{2,10},{10... | collective-permute-start | bytes 5308424 | tf_op jit(solution)/shard_map/ppermute | solution.py:620
  408.0 131.9 %all-to-all-start.5 = ((bf16[8,256,768]{2,1,0:T(8,128)(2,1)}), bf16[8,256,768]{2,1,0:T(8,128)(2,1)}, u32[]{:S(2)}, u32[]{:S(2)}) async-start(bf16[8,256,768]{2,1,0:T(8,128)(2,1)} %get-tuple-element.316), calls=%async_computation.5 | async-start | bytes 6291456 | tf_op jit(solution)/shard_map/all_to_all | solution.py:972
  449.8 39.8 %collective-permute-start.6 = (bf16[8,24,2304]{2,1,0:T(8,128)(2,1)S(1)}, bf16[8,24,2304]{2,1,0:T(8,128)(2,1)S(1)}, u32[]{:S(2)}, u32[]{:S(2)}) collective-permute-start(bf16[8,24,2304]{2,1,0:T(8,128)(2,1)S(1)} %bitcast.89), channel_id=1, source_target_pairs={{0,16},{8,24},{16,0},{24,8},{1,17},{9,25},{17,1},{25,9},{2,18},{10... | collective-permute-start | bytes 2654216 | tf_op jit(solution)/shard_map/ppermute | solution.py:620
  457.9 20.7 %copy-start.21 = (f32[512,768]{1,0:T(8,128)S(1)}, f32[512,768]{1,0:T(8,128)}, u32[]{:S(2)}) copy-start(f32[512,768]{1,0:T(8,128)} %get-tuple-element.274.after_ref) | copy-start | bytes 4718596
  457.9 20.7 %copy-start.25 = (bf16[512,768]{1,0:T(8,128)(2,1)S(1)}, bf16[512,768]{1,0:T(8,128)(2,1)}, u32[]{:S(2)}) copy-start(bf16[512,768]{1,0:T(8,128)(2,1)} %get-tuple-element.328.mix_ref.left1_ref) | copy-start | bytes 2359300
  457.9 20.7 %copy-start.30 = (bf16[512,768]{1,0:T(8,128)(2,1)S(1)}, bf16[512,768]{1,0:T(8,128)(2,1)}, u32[]{:S(2)}) copy-start(bf16[512,768]{1,0:T(8,128)(2,1)} %get-tuple-element.325.dq_ref.right1_ref) | copy-start | bytes 2359300
  457.9 20.7 %copy-start.44 = (bf16[512,2304]{1,0:T(8,128)(2,1)S(1)}, bf16[512,2304]{1,0:T(8,128)(2,1)}, u32[]{:S(2)}) copy-start(bf16[512,2304]{1,0:T(8,128)(2,1)} %get-tuple-element.327.qkv_ref) | copy-start | bytes 7077892
  457.9 20.7 %copy-start.46 = (f32[512,768]{1,0:T(8,128)S(1)}, f32[512,768]{1,0:T(8,128)}, u32[]{:S(2)}) copy-start(f32[512,768]{1,0:T(8,128)} %get-tuple-element.326.grad_cross_ref) | copy-start | bytes 4718596
  457.9 20.7 %copy-start.83 = (f32[6,4,256]{2,1,0:T(4,128)S(1)}, f32[6,4,256]{2,1,0:T(4,128)}, u32[]{:S(2)}) copy-start(f32[6,4,256]{2,1,0:T(4,128)} %get-tuple-element.329.lse_ref) | copy-start | bytes 73732
  508.8 5.7 collective-permute-start.7
  539.9 37.6 %collective-permute-start.8 = (bf16[8,24,3968]{2,1,0:T(8,128)(2,1)}, bf16[8,24,3968]{2,1,0:T(8,128)(2,1)}, u32[]{:S(2)}, u32[]{:S(2)}) collective-permute-start(bf16[8,24,3968]{2,1,0:T(8,128)(2,1)} %bitcast.21), channel_id=1, source_target_pairs={{0,16},{8,24},{16,0},{24,8},{1,17},{9,25},{17,1},{25,9},{2,18},{10... | collective-permute-start | bytes 4571144 | tf_op jit(solution)/shard_map/ppermute | solution.py:620
  541.9 103.6 %all-to-all-start.6 = ((bf16[8,128,768]{2,1,0:T(8,128)(2,1)}), bf16[8,128,768]{2,1,0:T(8,128)(2,1)S(1)}, u32[]{:S(2)}, u32[]{:S(2)}) async-start(bf16[8,128,768]{2,1,0:T(8,128)(2,1)} %get-tuple-element.361), calls=%async_computation.6 | async-start | bytes 3145728 | tf_op jit(solution)/shard_map/all_to_all | solution.py:972
  545.5 36.9 %copy-start.53 = (bf16[1,8,24,2304]{3,2,1,0:T(8,128)(2,1)S(1)}, bf16[1,8,24,2304]{3,2,1,0:T(8,128)(2,1)}, u32[]{:S(2)}) copy-start(bf16[1,8,24,2304]{3,2,1,0:T(8,128)(2,1)} %copy-done.52) | copy-start | bytes 2654212
  545.5 36.9 %copy-start.55 = (bf16[8,24,2304]{2,1,0:T(8,128)(2,1)S(1)}, bf16[8,24,2304]{2,1,0:T(8,128)(2,1)}, u32[]{:S(2)}) copy-start(bf16[8,24,2304]{2,1,0:T(8,128)(2,1)} %copy-done.54) | copy-start | bytes 2654212
  581.0 20.2 %collective-permute-start.9 = (bf16[4,24,3968]{2,1,0:T(8,128)(2,1)}, bf16[4,24,3968]{2,1,0:T(8,128)(2,1)S(1)}, u32[]{:S(2)}, u32[]{:S(2)}) collective-permute-start(bf16[4,24,3968]{2,1,0:T(8,128)(2,1)} %bitcast.28), channel_id=1, source_target_pairs={{0,1},{1,0},{2,3},{3,2},{4,5},{5,4},{6,7},{7,6},{8,9},{9,8},{10,11... | collective-permute-start | bytes 2285576 | tf_op jit(solution)/shard_map/ppermute | solution.py:620
  583.9 25.4 %collective-permute-start.12 = (bf16[4,24,2304]{2,1,0:T(8,128)(2,1)}, bf16[4,24,2304]{2,1,0:T(8,128)(2,1)S(1)}, u32[]{:S(2)}, u32[]{:S(2)}) collective-permute-start(bf16[4,24,2304]{2,1,0:T(8,128)(2,1)} %bitcast.40), channel_id=1, source_target_pairs={{0,1},{1,0},{2,3},{3,2},{4,5},{5,4},{6,7},{7,6},{8,9},{9,8},{10,11... | collective-permute-start | bytes 1327112 | tf_op jit(solution)/shard_map/ppermute | solution.py:620
  603.8 27.9 %collective-permute-start.10 = (bf16[2,24,3968]{2,1,0:T(8,128)(2,1)}, bf16[2,24,3968]{2,1,0:T(8,128)(2,1)S(1)}, u32[]{:S(2)}, u32[]{:S(2)}) collective-permute-start(bf16[2,24,3968]{2,1,0:T(8,128)(2,1)} %bitcast.31), channel_id=1, source_target_pairs={{0,2},{1,3},{2,0},{3,1},{4,6},{5,7},{6,4},{7,5},{8,10},{9,11},{10,... | collective-permute-start | bytes 1142792 | tf_op jit(solution)/shard_map/ppermute | solution.py:620
  609.4 8.3 %collective-permute-start.13 = (bf16[2,24,2304]{2,1,0:T(8,128)(2,1)S(1)}, bf16[2,24,2304]{2,1,0:T(8,128)(2,1)S(1)}, u32[]{:S(2)}, u32[]{:S(2)}) collective-permute-start(bf16[2,24,2304]{2,1,0:T(8,128)(2,1)S(1)} %bitcast.90), channel_id=1, source_target_pairs={{0,2},{1,3},{2,0},{3,1},{4,6},{5,7},{6,4},{7,5},{8,10},{9,11},{10,... | collective-permute-start | bytes 663560 | tf_op jit(solution)/shard_map/ppermute | solution.py:620
  617.8 6.9 %collective-permute-start.14 = (bf16[1,24,2304]{2,1,0:T(8,128)(2,1)S(1)}, bf16[1,24,2304]{2,1,0:T(8,128)(2,1)S(1)}, u32[]{:S(2)}, u32[]{:S(2)}) collective-permute-start(bf16[1,24,2304]{2,1,0:T(8,128)(2,1)S(1)} %bitcast.92), channel_id=1, source_target_pairs={{0,4},{1,5},{2,6},{3,7},{4,0},{5,1},{6,2},{7,3},{8,12},{9,13},{10,... | collective-permute-start | bytes 331784 | tf_op jit(solution)/shard_map/ppermute | solution.py:620
  631.8 15.4 %collective-permute-start.11 = (bf16[1,24,3968]{2,1,0:T(8,128)(2,1)S(1)}, bf16[1,24,3968]{2,1,0:T(8,128)(2,1)S(1)}, u32[]{:S(2)}, u32[]{:S(2)}) collective-permute-start(bf16[1,24,3968]{2,1,0:T(8,128)(2,1)S(1)} %bitcast.91), channel_id=1, source_target_pairs={{0,4},{1,5},{2,6},{3,7},{4,0},{5,1},{6,2},{7,3},{8,12},{9,13},{10,... | collective-permute-start | bytes 571400 | tf_op jit(solution)/shard_map/ppermute | solution.py:620
  (67 other events, 291.6 us)
Sparse Core Ops, SparseCore 0:
  13.1 81.3 all-gather.2
  98.1 120.4 all-gather.4
  356.7 210.4 reduce-scatter.1
